TPU v7x, 32 devices: a whole 2x2x4 slice. The times are simulated.
32 devices in a mesh: row: 4 (over z), col: 8 (over y, x, core).
Axes of the slice: x: 2, y: 2, z: 4, core: 2. Of those that a mesh axis runs over, the one named last changes fastest.
Arguments:
- velocity: bfloat16 [3, 8, 2048, 2048], P(None, 'col', 'row'), may hold values from -6 to 6
- vorticity: bfloat16 [3, 8, 2048, 2048], P(None, 'col', 'row'), may hold values from -6 to 6
- eddy_state: bfloat16 [8, 64, 3072], P('col', 'row'), may hold values from -0.359375 to 0.359375
- eddy_rate: bfloat16 [8, 64], P('col', 'row'), may hold values from 8 to 64
- block_owner: int32 [8, 4, 64, 1], P('col', 'row'), may hold values from 0 to 3; in each aligned block of 64 rows (0 to 63, 64 to 127, ..., all dimensions but the last counted through in order) at most 32 rows name the same one
- block_slot: int32 [8, 4, 64], P('col', 'row'), may hold values from 0 to 15
Outputs:
- spectral: float32 [3, 8, 1638400], P(None, None, ('row', 'col'))
Inputs may be any that keep to these rules, and one draw needn't show every extreme that they name: `block_owner`: among the 64 blocks of one DNS device, at most 32 have the same owner.
All inputs are finite; a program needn't handle non-finite values.
Results may differ from a plain program's by a relative error of at most 0.013.
Values may be sent and summed in bfloat16 or wider, within the bound.
A program may use at most 128 MiB of HBM per device.

v0:
```python
import math

import jax
import jax.numpy as jnp
from jax import lax
from jax.sharding import PartitionSpec as P

NX = 2048
NY = 2048
KXM = 640
KYM = 1280
RATIO = 4
BY = 8
BX = 128
S = 16
BLKV = 3072


section_step = 0.5
viscous_step = 0.15
vertical_step = 0.5


def padded_2(cells, sides, width):
    for axis, dim in sides:
        count = lax.axis_size(axis)
        head = lax.slice_in_dim(cells, 0, width, axis=dim)
        tail = lax.slice_in_dim(cells, cells.shape[dim] - width, cells.shape[dim], axis=dim)
        cells = jnp.concatenate(
            [
                lax.ppermute(tail, axis, [(i, (i + 1) % count) for i in range(count)]),
                cells,
                lax.ppermute(head, axis, [((i + 1) % count, i) for i in range(count)]),
            ],
            axis=dim,
        )
    return cells


def gauss_value(position, ratio):
    spread = 4.0 * ratio * ratio
    taps = jnp.arange(5 * ratio).astype(jnp.float32)
    shifted = taps - 2.0 * ratio - (ratio - 1) / 2.0
    total = jnp.sum(jnp.exp(-shifted * shifted / (2.0 * spread)))
    moved = position - 2.0 * ratio - (ratio - 1) / 2.0
    return jnp.exp(-moved * moved / (2.0 * spread)) / total


def x_weights(points, coarse, ratio):
    fine = jnp.arange(points, dtype=jnp.int32)[:, None]
    cells = jnp.arange(coarse, dtype=jnp.int32)[None, :]
    offset = jnp.mod(fine - ratio * cells + 2 * ratio, points)
    value = gauss_value(offset.astype(jnp.float32), ratio)
    return jnp.where(offset < 5 * ratio, value, 0.0).astype(jnp.bfloat16)


def y_weights(coarse, padded, ratio):
    cells = jnp.arange(coarse, dtype=jnp.int32)[:, None]
    fine = jnp.arange(padded, dtype=jnp.int32)[None, :]
    offset = fine - ratio * cells
    value = gauss_value(offset.astype(jnp.float32), ratio)
    return jnp.where((offset >= 0) & (offset < 5 * ratio), value, 0.0).astype(jnp.bfloat16)


def x_table(points, kept):
    fine = jnp.arange(points, dtype=jnp.int32)[:, None]
    column = jnp.arange(2 * kept, dtype=jnp.int32)[None, :]
    phase = jnp.mod(column // 2 * fine, points).astype(jnp.float32) * (2.0 * math.pi / points)
    value = jnp.where(column % 2 == 0, jnp.cos(phase), -jnp.sin(phase))
    return (value / math.sqrt(points)).astype(jnp.bfloat16)


def y_tables(points, kept, first, count):
    fine = jnp.arange(points, dtype=jnp.int32)[:, None]
    wave = jnp.arange(count, dtype=jnp.int32)[None, :] + (first - kept // 2)
    phase = jnp.mod(wave * fine, points).astype(jnp.float32) * (2.0 * math.pi / points)
    scale = 1.0 / math.sqrt(points)
    return (
        (jnp.cos(phase) * scale).astype(jnp.bfloat16),
        (jnp.sin(phase) * scale).astype(jnp.bfloat16),
    )


def vertical_inverse(planes):
    index = jnp.arange(planes)
    ends = (index == 0) | (index == planes - 1)
    diagonal = jnp.where(ends, 1.0 + vertical_step, 1.0 + 2.0 * vertical_step).astype(jnp.float32)
    lower = jnp.where(index == 0, 0.0, -vertical_step).astype(jnp.float32)
    upper = jnp.where(index == planes - 1, 0.0, -vertical_step).astype(jnp.float32)
    return lax.linalg.tridiagonal_solve(lower, diagonal, upper, jnp.eye(planes, dtype=jnp.float32))


def damping(x_wave, y_wave, points_x, points_y):
    angle_x = x_wave.astype(jnp.float32) * (2.0 * math.pi / points_x)
    angle_y = y_wave.astype(jnp.float32) * (2.0 * math.pi / points_y)
    total = (
        angle_y[:, None, None] * angle_y[:, None, None]
        + angle_x[None, None, :] * angle_x[None, None, :]
    )
    return jnp.broadcast_to(jnp.exp(-viscous_step * total), (y_wave.shape[0], 2, x_wave.shape[0]))


def along_y(piece):
    items, width, length = piece.shape
    half = width // 2
    split = piece.reshape(items, half, 2, length)
    real_in = split[:, :, 0, :]
    imag_in = split[:, :, 1, :]
    block = 256
    outputs = []
    for first in range(0, KYM, block):
        cosine, sine = y_tables(length, KYM, first, block)
        real_out = jnp.einsum(
            "kin,nj->kji", real_in, cosine, preferred_element_type=jnp.float32
        ) + jnp.einsum("kin,nj->kji", imag_in, sine, preferred_element_type=jnp.float32)
        imag_out = jnp.einsum(
            "kin,nj->kji", imag_in, cosine, preferred_element_type=jnp.float32
        ) - jnp.einsum("kin,nj->kji", real_in, sine, preferred_element_type=jnp.float32)
        outputs.append(jnp.concatenate([real_out, imag_out], axis=2))
    return jnp.concatenate(outputs, axis=1).astype(jnp.bfloat16)


def per_device(velocity, vorticity, eddy_state, eddy_rate, block_owner, block_slot):
    components, depth, rows, points = velocity.shape
    coarse_rows = rows // RATIO
    coarse_cols = points // RATIO
    xweights = x_weights(points, coarse_cols, RATIO)
    local = jnp.einsum(
        "czyn,nx->czyx", velocity, xweights, preferred_element_type=jnp.float32
    ).astype(jnp.bfloat16)
    along = padded_2(local, (("row", 2),), 2 * RATIO)
    yweights = y_weights(coarse_rows, rows + 4 * RATIO, RATIO)
    filtered = jnp.einsum(
        "iy,czyx->czix", yweights, along, preferred_element_type=jnp.float32
    ).astype(jnp.bfloat16)
    ybands = coarse_rows // BY
    xbands = coarse_cols // BX
    count = depth * ybands * xbands
    blocks = filtered.reshape(components, depth, ybands, BY, xbands, BX).transpose(1, 2, 4, 0, 3, 5)
    blocks = blocks.reshape(count, BLKV)
    owners = block_owner.reshape(count)
    slots = block_slot.reshape(count)
    owners_total = lax.axis_size("row")
    every_state, every_rate = (
        lax.all_gather(eddy_state, "row", axis=1, tiled=True),
        lax.all_gather(eddy_rate, "row", axis=1, tiled=True),
    )
    chosen = owners * S + slots
    lookup = (chosen[:, None] == jnp.arange(owners_total * S, dtype=jnp.int32)[None, :]).astype(
        jnp.bfloat16
    )
    state = jnp.dot(lookup, every_state[0], preferred_element_type=jnp.float32)
    rates = jnp.dot(lookup, every_rate[0][:, None], preferred_element_type=jnp.float32)[:, 0]
    forcing_blocks = (rates[:, None] * (state - blocks.astype(jnp.float32))).astype(jnp.bfloat16)
    coarse = forcing_blocks.reshape(depth, ybands, xbands, components, BY, BX).transpose(
        3, 0, 1, 4, 2, 5
    )
    coarse = coarse.reshape(components, depth, coarse_rows, coarse_cols).astype(jnp.float32)
    forcing = jnp.repeat(jnp.repeat(coarse, RATIO, axis=2), RATIO, axis=3)
    speed = velocity.astype(jnp.float32)
    spin = vorticity.astype(jnp.float32)
    cross = jnp.stack(
        [
            speed[1] * spin[2] - speed[2] * spin[1],
            speed[2] * spin[0] - speed[0] * spin[2],
            speed[0] * spin[1] - speed[1] * spin[0],
        ],
        axis=0,
    )
    section = (speed + section_step * (cross + forcing)).astype(jnp.bfloat16)
    xtable = x_table(points, KXM)
    spectrum = jnp.einsum(
        "kyn,nm->kmy",
        section.reshape(components * depth, rows, points),
        xtable,
        preferred_element_type=jnp.float32,
    ).astype(jnp.bfloat16)
    ordered = along_y(lax.all_to_all(spectrum, "row", split_axis=1, concat_axis=2, tiled=True))
    ordered = ordered.reshape(components, depth, KYM, -1)
    inverse = vertical_inverse(depth * lax.axis_size("col")).astype(jnp.bfloat16)
    mode_rows = KYM // lax.axis_size("col")
    mode_cols = ordered.shape[3] // 2
    x_wave = lax.axis_index("row") * mode_cols + jnp.arange(mode_cols, dtype=jnp.int32)
    y_wave = lax.axis_index("col") * mode_rows + jnp.arange(mode_rows, dtype=jnp.int32) - KYM // 2
    factor = damping(x_wave, y_wave, NX, NY).reshape(-1)
    piece = lax.all_to_all(ordered, "col", split_axis=2, concat_axis=1, tiled=True)
    items = piece.shape[0]
    flat = piece.reshape(items, piece.shape[1], -1)
    mixed = jnp.einsum("wz,kzl->kwl", inverse, flat, preferred_element_type=jnp.float32)
    return mixed * factor[None, None, :]


def solution(mesh):
    return jax.shard_map(
        per_device,
        mesh=mesh,
        in_specs=(
            P(None, "col", "row", None),
            P(None, "col", "row", None),
            P("col", "row", None),
            P("col", "row"),
            P("col", "row", None, None),
            P("col", "row", None),
        ),
        out_specs=P(None, None, ("row", "col")),
        check_vma=False,
    )
```

profile of v0, /device:TPU:0, one launch (start us, length us, event | category | flops | bytes accessed | tf_op | source)
XLA Modules:
  0.0 582.2 jit_solution(14752560193493699065)
XLA Ops:
  13.9 8.7 %copy.30 = bf16[3,1,512,2048]{2,3,0,1:T(8,128)(2,1)} copy(bf16[3,1,512,2048]{3,2,1,0:T(8,128)(2,1)} %param.6) | data formatting | bytes 12582912 | tf_op args[0]
  24.1 10.3 %all-reduce = bf16[64]{0:T(256)(128)(2,1)S(1)} all-reduce(bf16[64]{0:T(256)(128)(2,1)S(1)} %dynamic-update-slice), channel_id=1, replica_groups=mesh['row'=4,'col'=8] {'row'}, use_global_device_ids=true, to_apply=%add | all-reduce | flops 64 | bytes 256 | tf_op jit(solution)/shard_map/reshape
  34.4 14.6 %all_gather.7 = bf16[1,64,3072]{2,1,0:T(8,128)(2,1)S(1)} all-gather(bf16[1,16,3072]{2,1,0:T(8,128)(2,1)S(1)} %copy-done.1), channel_id=1, replica_groups=mesh['row'=4,'col'=8] {'row'}, dimensions={1}, use_global_device_ids=true | all-gather | bytes 491520 | tf_op jit(solution)/shard_map/all_gather | solution.py:145
  49.1 9.2 %convert_element_type.226 = f32[3,1,512,2048]{2,3,0,1:T(8,128)} convert(bf16[3,1,512,2048]{2,3,0,1:T(8,128)(2,1)} %copy.30) | non-fusion elementwise | flops 3145728 | bytes 18874368 | tf_op jit(solution)/shard_map/convert_element_type | solution.py:160
  58.3 8.6 %copy.31 = bf16[3,1,512,2048]{2,3,0,1:T(8,128)(2,1)} copy(bf16[3,1,512,2048]{3,2,1,0:T(8,128)(2,1)} %param.7) | data formatting | bytes 12582912 | tf_op args[1]
  66.8 9.7 %convert_element_type.227 = f32[3,1,512,2048]{2,3,0,1:T(8,128)} convert(bf16[3,1,512,2048]{2,3,0,1:T(8,128)(2,1)} %copy.31) | non-fusion elementwise | flops 3145728 | bytes 18874368 | tf_op jit(solution)/shard_map/convert_element_type | solution.py:161
  76.7 10.0 %multiply_subtract_fusion.2 = (f32[1,1,512,2048]{2,3,0,1:T(8,128)}, f32[1,1,512,2048]{2,3,0,1:T(8,128)}, f32[1,1,512,2048]{2,3,0,1:T(8,128)}) fusion(f32[3,1,512,2048]{2,3,0,1:T(8,128)} %convert_element_type.227, f32[3,1,512,2048]{2,3,0,1:T(8,128)S(1)} %copy-done), kind=kLoop, calls=%fused_computation.41 | loop fusion | flops 9437184 | bytes 37748736 | tf_op jit(solution)/shard_map/sub | solution.py:164
  86.8 45.1 %fusion.364 = bf16[2048,1280,1]{0,1,2:T(8,128)(2,1)} fusion(s32[1280]{0:T(1024)S(1)} %add_select_fusion.7, pred[1280]{0:T(1024)(128)(4,1)S(1)} %fusion.192), kind=kLoop, calls=%fused_computation.25.clone.clone.clone.clone.clone.clone.2 | loop fusion | flops 47185920 | bytes 5249280 | tf_op jit(solution)/shard_map/kyn,nm->kmy/dot_general | solution.py:172
  149.9 14.7 %broadcast_in_dim.48 = f32[3,1,512,2048]{2,3,0,1:T(8,128)} reshape(f32[3,512,512,4]{1,3,2,0:T(4,128)} %broadcast_in_dim.47) | data formatting | bytes 25165824 | tf_op jit(solution)/shard_map/broadcast_in_dim | solution.py:159
  164.5 17.5 %fusion.36 = bf16[3,1280,512]{2,1,0:T(8,128)(2,1)S(1)} fusion(f32[3,1,512,2048]{2,3,0,1:T(8,128)} %broadcast_in_dim.48, f32[1,1,512,2048]{2,3,0,1:T(8,128)} %get-tuple-element.22, f32[1,1,512,2048]{2,3,0,1:T(8,128)} %get-tuple-element.21, f32[1,1,512,2048]{2,3,0,1:T(8,128)} %get-tuple-element.20, bf16[3,1,512,2048]{2,3,0,1:T(8,128)(2,1)} %copy.30, ...), kind=kOutput, calls=%fused_computation.44 | convolution fusion | flops 8077049856 | bytes 40632320 | tf_op jit(solution)/shard_map/kyn,nm->kmy/dot_general | solution.py:172
  182.0 17.5 %copy.37 = bf16[3,1280,512]{2,0,1:T(4,128)(2,1)} copy(bf16[3,1280,512]{2,1,0:T(8,128)(2,1)S(1)} %fusion.36) | data formatting | bytes 7864320 | tf_op jit(solution)/shard_map/convert_element_type | solution.py:177
  204.6 111.3 %all-to-all-done = bf16[3,1280,512]{2,0,1:T(4,128)(2,1)} async-done(((bf16[3,1280,512]{2,0,1:T(4,128)(2,1)}), bf16[3,1280,512]{2,0,1:T(4,128)(2,1)}, u32[]{:S(2)}, u32[]{:S(2)}) %all-to-all-start) | async-done | bytes 3932192 | tf_op jit(solution)/shard_map/all_to_all | solution.py:178
  324.0 10.0 %reshape.376 = bf16[3,160,2,2048]{3,2,1,0:T(2,128)(2,1)} reshape(bf16[3,320,4,512]{3,2,1,0:T(4,128)(2,1)} %bitcast.237) | data formatting | bytes 7864320 | tf_op jit(solution)/shard_map/reshape | solution.py:106
  334.0 8.6 %fusion.332 = (bf16[3,160,1,2048]{3,2,1,0:T(2,128)(2,1)S(1)}, bf16[3,160,1,2048]{3,2,1,0:T(2,128)(2,1)S(1)}) fusion(bf16[3,160,2,2048]{3,2,1,0:T(2,128)(2,1)} %reshape.376), kind=kLoop, calls=%fused_computation.391 | loop fusion | bytes 7864320 | tf_op jit(solution)/shard_map/slice | solution.py:107
  353.1 8.2 %fusion.163 = f32[256,3,160]{0,2,1:T(8,128)S(1)} fusion(bf16[3,160,2048]{2,1,0:T(8,128)(2,1)S(1)} %get-tuple-element.52, s32[256]{0:T(256)S(1)} %iota_add_fusion.4), kind=kOutput, calls=%fused_computation.180 | convolution fusion | flops 511705088 | bytes 2458624 | tf_op jit(solution)/shard_map/kin,nj->kji/dot_general | solution.py:116
  361.3 8.4 %fusion.159 = f32[256,3,160]{0,2,1:T(8,128)S(1)} fusion(bf16[3,160,2048]{2,1,0:T(8,128)(2,1)S(1)} %get-tuple-element.53, s32[256]{0:T(256)S(1)} %iota_add_fusion.3), kind=kOutput, calls=%fused_computation.179 | convolution fusion | flops 511705088 | bytes 2458624 | tf_op jit(solution)/shard_map/kin,nj->kji/dot_general | solution.py:113
  369.7 8.1 %fusion.157 = f32[256,3,160]{0,2,1:T(8,128)S(1)} fusion(bf16[3,160,2048]{2,1,0:T(8,128)(2,1)S(1)} %get-tuple-element.52, s32[256]{0:T(256)S(1)} %iota_add_fusion.3), kind=kOutput, calls=%fused_computation.178 | convolution fusion | flops 511705088 | bytes 2458624 | tf_op jit(solution)/shard_map/kin,nj->kji/dot_general | solution.py:116
  385.8 8.2 %fusion.151 = f32[256,3,160]{0,2,1:T(8,128)S(1)} fusion(bf16[3,160,2048]{2,1,0:T(8,128)(2,1)S(1)} %get-tuple-element.52, s32[256]{0:T(256)S(1)} %iota_add_fusion.2), kind=kOutput, calls=%fused_computation.176 | convolution fusion | flops 511705088 | bytes 2458624 | tf_op jit(solution)/shard_map/kin,nj->kji/dot_general | solution.py:116
  394.0 8.4 %fusion.147 = f32[256,3,160]{0,2,1:T(8,128)S(1)} fusion(bf16[3,160,2048]{2,1,0:T(8,128)(2,1)S(1)} %get-tuple-element.53, s32[256]{0:T(256)S(1)} %iota_add_fusion.1), kind=kOutput, calls=%fused_computation.175 | convolution fusion | flops 511705088 | bytes 2458624 | tf_op jit(solution)/shard_map/kin,nj->kji/dot_general | solution.py:113
  410.4 8.1 %fusion.141 = f32[256,3,160]{0,2,1:T(8,128)S(1)} fusion(bf16[3,160,2048]{2,1,0:T(8,128)(2,1)S(1)} %get-tuple-element.53, s32[256]{0:T(256)S(1)} %iota_add_fusion), kind=kOutput, calls=%fused_computation.173 | convolution fusion | flops 511705088 | bytes 2458624 | tf_op jit(solution)/shard_map/kin,nj->kji/dot_general | solution.py:113
  418.5 8.2 %fusion.139 = f32[256,3,160]{0,2,1:T(8,128)S(1)} fusion(bf16[3,160,2048]{2,1,0:T(8,128)(2,1)S(1)} %get-tuple-element.52, s32[256]{0:T(256)S(1)} %iota_add_fusion), kind=kOutput, calls=%fused_computation.172 | convolution fusion | flops 511705088 | bytes 2458624 | tf_op jit(solution)/shard_map/kin,nj->kji/dot_general | solution.py:116
  426.7 8.6 %fusion.126 = bf16[3,256,160]{1,2,0:T(8,128)(2,1)S(1)} fusion(f32[256,3,160]{0,2,1:T(8,128)S(1)} %fusion.165, bf16[3,160,2048]{2,1,0:T(8,128)(2,1)S(1)} %get-tuple-element.52, s32[256]{0:T(256)S(1)} %iota_add_fusion.4), kind=kOutput, calls=%fused_computation.160 | convolution fusion | flops 511950848 | bytes 2704384 | tf_op jit(solution)/shard_map/kin,nj->kji/dot_general | solution.py:115
  435.3 8.5 %fusion.125 = bf16[3,256,160]{1,2,0:T(8,128)(2,1)S(1)} fusion(f32[256,3,160]{0,2,1:T(8,128)S(1)} %fusion.163, bf16[3,160,2048]{2,1,0:T(8,128)(2,1)S(1)} %get-tuple-element.53, s32[256]{0:T(256)S(1)} %iota_add_fusion.4), kind=kOutput, calls=%fused_computation.159 | convolution fusion | flops 511950848 | bytes 2704384 | tf_op jit(solution)/shard_map/kin,nj->kji/dot_general | solution.py:118
  443.8 9.0 %fusion.124 = bf16[3,256,160]{1,2,0:T(8,128)(2,1)S(1)} fusion(f32[256,3,160]{0,2,1:T(8,128)S(1)} %fusion.159, bf16[3,160,2048]{2,1,0:T(8,128)(2,1)S(1)} %get-tuple-element.52, s32[256]{0:T(256)S(1)} %iota_add_fusion.3), kind=kOutput, calls=%fused_computation.158 | convolution fusion | flops 511950848 | bytes 2704384 | tf_op jit(solution)/shard_map/kin,nj->kji/dot_general | solution.py:115
  452.8 8.5 %fusion.123 = bf16[3,256,160]{1,2,0:T(8,128)(2,1)S(1)} fusion(f32[256,3,160]{0,2,1:T(8,128)S(1)} %fusion.157, bf16[3,160,2048]{2,1,0:T(8,128)(2,1)S(1)} %get-tuple-element.53, s32[256]{0:T(256)S(1)} %iota_add_fusion.3), kind=kOutput, calls=%fused_computation.157 | convolution fusion | flops 511950848 | bytes 2704384 | tf_op jit(solution)/shard_map/kin,nj->kji/dot_general | solution.py:118
  461.3 8.7 %fusion.122 = bf16[3,256,160]{1,2,0:T(8,128)(2,1)S(1)} fusion(f32[256,3,160]{0,2,1:T(8,128)S(1)} %fusion.153, bf16[3,160,2048]{2,1,0:T(8,128)(2,1)S(1)} %get-tuple-element.52, s32[256]{0:T(256)S(1)} %iota_add_fusion.2), kind=kOutput, calls=%fused_computation.156 | convolution fusion | flops 511950848 | bytes 2704384 | tf_op jit(solution)/shard_map/kin,nj->kji/dot_general | solution.py:115
  470.0 8.5 %fusion.121 = bf16[3,256,160]{1,2,0:T(8,128)(2,1)S(1)} fusion(f32[256,3,160]{0,2,1:T(8,128)S(1)} %fusion.151, bf16[3,160,2048]{2,1,0:T(8,128)(2,1)S(1)} %get-tuple-element.53, s32[256]{0:T(256)S(1)} %iota_add_fusion.2), kind=kOutput, calls=%fused_computation.155 | convolution fusion | flops 511950848 | bytes 2704384 | tf_op jit(solution)/shard_map/kin,nj->kji/dot_general | solution.py:118
  478.5 8.8 %fusion.120 = bf16[3,256,160]{1,2,0:T(8,128)(2,1)S(1)} fusion(f32[256,3,160]{0,2,1:T(8,128)S(1)} %fusion.147, bf16[3,160,2048]{2,1,0:T(8,128)(2,1)S(1)} %get-tuple-element.52, s32[256]{0:T(256)S(1)} %iota_add_fusion.1), kind=kOutput, calls=%fused_computation.154 | convolution fusion | flops 511950848 | bytes 2704384 | tf_op jit(solution)/shard_map/kin,nj->kji/dot_general | solution.py:115
  487.3 8.5 %fusion.119 = bf16[3,256,160]{1,2,0:T(8,128)(2,1)S(1)} fusion(f32[256,3,160]{0,2,1:T(8,128)S(1)} %fusion.145, bf16[3,160,2048]{2,1,0:T(8,128)(2,1)S(1)} %get-tuple-element.53, s32[256]{0:T(256)S(1)} %iota_add_fusion.1), kind=kOutput, calls=%fused_computation.153 | convolution fusion | flops 511950848 | bytes 2704384 | tf_op jit(solution)/shard_map/kin,nj->kji/dot_general | solution.py:118
  495.8 8.8 %fusion.118 = bf16[3,256,160]{1,2,0:T(8,128)(2,1)S(1)} fusion(f32[256,3,160]{0,2,1:T(8,128)S(1)} %fusion.141, bf16[3,160,2048]{2,1,0:T(8,128)(2,1)S(1)} %get-tuple-element.52, s32[256]{0:T(256)S(1)} %iota_add_fusion), kind=kOutput, calls=%fused_computation.152 | convolution fusion | flops 511950848 | bytes 2704384 | tf_op jit(solution)/shard_map/kin,nj->kji/dot_general | solution.py:115
  504.7 8.5 %fusion.117 = bf16[3,256,160]{1,2,0:T(8,128)(2,1)S(1)} fusion(f32[256,3,160]{0,2,1:T(8,128)S(1)} %fusion.139, bf16[3,160,2048]{2,1,0:T(8,128)(2,1)S(1)} %get-tuple-element.53, s32[256]{0:T(256)S(1)} %iota_add_fusion), kind=kOutput, calls=%fused_computation.151 | convolution fusion | flops 511950848 | bytes 2704384 | tf_op jit(solution)/shard_map/kin,nj->kji/dot_general | solution.py:118
  545.9 24.7 %all-to-all-done.1 = bf16[3,1,1280,320]{3,0,1,2:T(4,128)(2,1)} async-done(((bf16[3,1,1280,320]{3,0,1,2:T(4,128)(2,1)}), bf16[3,1,1280,320]{3,0,1,2:T(4,128)(2,1)}, u32[]{:S(2)}, u32[]{:S(2)}) %all-to-all-start.1) | async-done | bytes 2457632 | tf_op jit(solution)/shard_map/all_to_all | solution.py:186
  (77 shorter events, 102.4 us)
Async XLA Ops:
  8.7 123.2 %collective-permute-start = (bf16[3,1,8,512]{3,2,0,1:T(8,128)(2,1)S(1)}, bf16[3,1,8,512]{3,2,0,1:T(8,128)(2,1)S(1)}, u32[]{:S(2)}, u32[]{:S(2)}) collective-permute-start(bf16[3,1,8,512]{3,2,0,1:T(8,128)(2,1)S(1)} %get-tuple-element.25), channel_id=1, source_target_pairs={{0,8},{8,16},{16,24},{24,0},{1,9},{9,17},{17,25},{25,1},{2,10},{10... | collective-permute-start | bytes 73736 | tf_op jit(solution)/shard_map/ppermute | solution.py:31
  11.8 120.1 %collective-permute-start.1 = (bf16[3,1,8,512]{3,2,0,1:T(8,128)(2,1)S(1)}, bf16[3,1,8,512]{3,2,0,1:T(8,128)(2,1)S(1)}, u32[]{:S(2)}, u32[]{:S(2)}) collective-permute-start(bf16[3,1,8,512]{3,2,0,1:T(8,128)(2,1)S(1)} %get-tuple-element.26), channel_id=1, source_target_pairs={{8,0},{16,8},{24,16},{0,24},{9,1},{17,9},{25,17},{1,25},{10,2},{18... | collective-permute-start | bytes 73736 | tf_op jit(solution)/shard_map/ppermute | solution.py:33
  13.9 8.7 %copy-start.5 = (u32[32]{0:T(128)S(1)}, u32[32]{0:T(128)}, u32[]{:S(2)}) copy-start(u32[32]{0:T(128)} %constant.167) | copy-start | bytes 388
  13.9 10.0 %copy-start.2 = (bf16[1,16]{1,0:T(2,128)(2,1)S(1)}, bf16[1,16]{1,0:T(2,128)(2,1)}, u32[]{:S(2)}) copy-start(bf16[1,16]{1,0:T(2,128)(2,1)} %param.9) | copy-start | bytes 100
  13.9 20.6 %copy-start.1 = (bf16[1,16,3072]{2,1,0:T(8,128)(2,1)S(1)}, bf16[1,16,3072]{2,1,0:T(8,128)(2,1)}, u32[]{:S(2)}) copy-start(bf16[1,16,3072]{2,1,0:T(8,128)(2,1)} %param.8) | copy-start | bytes 294916
  66.8 9.7 %copy-start.3 = (s32[1,1,64]{2,1,0:T(1,128)S(1)}, s32[1,1,64]{2,1,0:T(1,128)}, u32[]{:S(2)}) copy-start(s32[1,1,64]{2,1,0:T(1,128)} %param.11) | copy-start | bytes 772
  66.8 9.7 %copy-start.4 = (s32[1,1,64,1]{2,3,1,0:T(1,128)S(1)}, s32[1,1,64,1]{2,3,1,0:T(1,128)}, u32[]{:S(2)}) copy-start(s32[1,1,64,1]{2,3,1,0:T(1,128)} %param.10) | copy-start | bytes 772
  66.8 9.9 %copy-start = (f32[3,1,512,2048]{2,3,0,1:T(8,128)S(1)}, f32[3,1,512,2048]{2,3,0,1:T(8,128)}, u32[]{:S(2)}) copy-start(f32[3,1,512,2048]{2,3,0,1:T(8,128)} %convert_element_type.226) | copy-start | bytes 37748740
  199.5 116.4 %all-to-all-start = ((bf16[3,1280,512]{2,0,1:T(4,128)(2,1)}), bf16[3,1280,512]{2,0,1:T(4,128)(2,1)}, u32[]{:S(2)}, u32[]{:S(2)}) async-start(bf16[3,1280,512]{2,0,1:T(4,128)(2,1)} %copy.37), calls=%async_computation | async-start | bytes 10485760 | tf_op jit(solution)/shard_map/all_to_all | solution.py:178
  519.4 51.1 %all-to-all-start.1 = ((bf16[3,1,1280,320]{3,0,1,2:T(4,128)(2,1)}), bf16[3,1,1280,320]{3,0,1,2:T(4,128)(2,1)}, u32[]{:S(2)}, u32[]{:S(2)}) async-start(bf16[3,1,1280,320]{3,0,1,2:T(4,128)(2,1)} %copy.41), calls=%async_computation.1 | async-start | bytes 7864320 | tf_op jit(solution)/shard_map/all_to_all | solution.py:186
where the time goes:
time: 589 us; the launch traced here: 582 us
  matrix products  200 us (34%)
  waiting for transfers between devices  136 us (23%)
  local copies, waits for them, and re-layouts  111 us (19%)
  other arithmetic  80.1 us (14%)
  blocking collectives  24.9 us (4%)
  between operations  15.4 us (3%)
  starting transfers between devices  15.1 us (3%)
    all_to_all x1, waiting for transfers between devices, per_device(): lax.all_to_all(spectrum, 'row', split_axis=1, concat_axis=2, tiled=True)  111 us
    dot_general x1, other arithmetic, per_device(): jnp.einsum('kyn,nm->kmy', section.reshape(components * depth, rows, point...  45.1 us
    dot_general x5, matrix products, along_y(): jnp.einsum('kin,nj->kji', imag_in, sine, preferred_element_type=jnp.float32)  43.9 us
    dot_general x5, matrix products, along_y(): jnp.einsum('kin,nj->kji', real_in, sine, preferred_element_type=jnp.float32)  42.5 us
    dot_general x5, matrix products, along_y(): jnp.einsum('kin,nj->kji', real_in, cosine, preferred_element_type=jnp.flo...  40.9 us
    dot_general x5, matrix products, along_y(): jnp.einsum('kin,nj->kji', imag_in, cosine, preferred_element_type=jnp.flo...  40.7 us
    broadcast_in_dim x5, local copies, waits for them, and re-layouts, per_device(): forcing = jnp.repeat(jnp.repeat(coarse, RATIO, axis=2), RATIO, axis=3)  30.2 us
    all_to_all x1, waiting for transfers between devices, per_device(): lax.all_to_all(ordered, 'col', split_axis=2, concat_axis=1, tiled=True)  24.7 us
  transfers between devices with their start and end apart: 4, of which 2 were waited for; matrix products, arithmetic and copies ran while one was open for 17% of the time, Pallas kernels for 0%

commit v1 on v0

--- a/solution.py
+++ b/solution.py
@@ -2,7 +2,10 @@
 
 import jax
 import jax.numpy as jnp
+import numpy as np
 from jax import lax
+from jax.experimental import pallas as pl
+from jax.experimental.pallas import tpu as pltpu
 from jax.sharding import PartitionSpec as P
 
 NX = 2048
@@ -120,7 +123,7 @@
     return jnp.concatenate(outputs, axis=1).astype(jnp.bfloat16)
 
 
-def per_device(velocity, vorticity, eddy_state, eddy_rate, block_owner, block_slot):
+def generic_device(velocity, vorticity, eddy_state, eddy_rate, block_owner, block_slot):
     components, depth, rows, points = velocity.shape
     coarse_rows = rows // RATIO
     coarse_cols = points // RATIO
@@ -190,6 +193,244 @@
     return mixed * factor[None, None, :]
 
 
+F32 = jnp.float32
+BF16 = jnp.bfloat16
+YB = 256
+NT = (((1,), (1,)), ((), ()))
+
+
+def fits(rows, points, n_row, n_col):
+    mode_cols, mode_rows = KXM // n_row, KYM // n_col
+    return (
+        n_row == 4
+        and rows % YB == 0
+        and points % 512 == 0
+        and mode_cols % 16 == 0
+        and (2 * mode_cols) % 128 == 64
+        and mode_rows % 32 == 0
+        and n_col % 8 == 0
+    )
+
+
+def x_tables_t(points, kept, n_row):
+    per = kept // n_row
+    row = np.arange(2 * kept)
+    wave = row // (2 * per) * per + row % per
+    imag = row // per % 2
+    phase = (wave[:, None] * np.arange(points)[None, :]) % points * (2.0 * math.pi / points)
+    value = np.where(imag[:, None] == 0, np.cos(phase), -np.sin(phase)) / math.sqrt(points)
+    fine = value.astype(BF16)
+    coarse = section_step * fine.astype(np.float32).reshape(2 * kept, points // RATIO, RATIO).sum(2)
+    return fine, coarse.astype(BF16)
+
+
+def y_tables_t(points, kept, quarter):
+    s = np.arange(kept // 4)
+    out = []
+    for q in range(4):
+        wave = 4 * s + q - kept // 2
+        phase = (wave[:, None] * np.arange(quarter)[None, :]) % points * (2.0 * math.pi / points)
+        out.append(np.concatenate([np.cos(phase), np.sin(phase)], axis=1) / math.sqrt(points))
+    return np.stack(out).astype(BF16)
+
+
+def x_kernel(comp, vel_ref, vort_ref, coarse_ref, xt_ref, xc_ref, out_ref):
+    b, c = (comp + 1) % 3, (comp + 2) % 3
+    section = (
+        vel_ref[comp].astype(F32)
+        + section_step
+        * (
+            vel_ref[b].astype(F32) * vort_ref[c].astype(F32)
+            - vel_ref[c].astype(F32) * vort_ref[b].astype(F32)
+        )
+    ).astype(BF16)
+    yb = section.shape[0]
+    fine = lax.broadcasted_iota(jnp.int32, (yb, yb // RATIO), 0) // RATIO
+    cell = lax.broadcasted_iota(jnp.int32, (yb, yb // RATIO), 1)
+    spread = jnp.where(fine == cell, 1.0, 0.0).astype(BF16)
+    repeated = jnp.dot(spread, coarse_ref[0], preferred_element_type=F32).astype(BF16)
+    dests, width, _ = out_ref.shape
+    for r in range(dests):
+        lines = slice(r * width, (r + 1) * width)
+        total = lax.dot_general(xt_ref[lines, :], section, NT, preferred_element_type=F32)
+        total += lax.dot_general(xc_ref[lines, :], repeated, NT, preferred_element_type=F32)
+        out_ref[r] = total.astype(BF16)
+
+
+def x_stage(comp, vel, vort, coarse, xt, xc, n_row):
+    _, rows, points = vel.shape
+    width = xt.shape[0] // n_row
+    full = lambda a: pl.BlockSpec(a.shape, lambda i: (0,) * a.ndim)
+    return pl.pallas_call(
+        lambda *refs: x_kernel(comp, *refs),
+        out_shape=jax.ShapeDtypeStruct((n_row, width, rows), BF16),
+        grid=(rows // YB,),
+        in_specs=[
+            pl.BlockSpec((3, YB, points), lambda i: (0, i, 0)),
+            pl.BlockSpec((3, YB, points), lambda i: (0, i, 0)),
+            pl.BlockSpec((1, YB // RATIO, points // RATIO), lambda i: (comp, i, 0)),
+            full(xt),
+            full(xc),
+        ],
+        out_specs=pl.BlockSpec((n_row, width, YB), lambda i: (0, 0, i)),
+        cost_estimate=pl.CostEstimate(
+            flops=2 * rows * xt.shape[0] * (points + points // RATIO),
+            bytes_accessed=20 * rows * points,
+            transcendentals=0,
+        ),
+        compiler_params=pltpu.CompilerParams(vmem_limit_bytes=56 * 2**20),
+        name="x_stage",
+    )(vel, vort, coarse, xt, xc)
+
+
+def y_kernel(in_ref, tab_ref, out_ref):
+    half = in_ref.shape[1] // 2
+    a = [in_ref[r, :half, :].astype(F32) for r in range(4)]
+    b = [in_ref[r, half:, :].astype(F32) for r in range(4)]
+    a02, a13, b02, b13 = a[0] + a[2], a[1] + a[3], b[0] + b[2], b[1] + b[3]
+    d02, d13, e02, e13 = a[0] - a[2], a[1] - a[3], b[0] - b[2], b[1] - b[3]
+    real = [a02 + a13, d02 + e13, a02 - a13, d02 - e13]
+    imag = [b02 + b13, e02 - d13, b02 - b13, e02 + d13]
+    results = []
+    for q in range(4):
+        re, im = real[q].astype(BF16), imag[q].astype(BF16)
+        turned = jnp.concatenate(
+            [jnp.concatenate([re, im], axis=0), jnp.concatenate([im, -re], axis=0)], axis=1
+        )
+        results.append(lax.dot_general(tab_ref[q], turned, NT, preferred_element_type=F32))
+    dests, lines, _ = out_ref.shape
+    part = lines // 4
+    for d in range(dests):
+        out_ref[d] = jnp.concatenate(
+            [results[q][d * part : (d + 1) * part] for q in range(4)], axis=0
+        ).astype(BF16)
+
+
+def y_stage(piece, tab, n_col):
+    _, width, quarter = piece.shape
+    lines = 4 * tab.shape[1] // n_col
+    return pl.pallas_call(
+        y_kernel,
+        out_shape=jax.ShapeDtypeStruct((n_col, lines, width), BF16),
+        cost_estimate=pl.CostEstimate(
+            flops=2 * tab.size * width, bytes_accessed=8 * tab.size, transcendentals=0
+        ),
+        compiler_params=pltpu.CompilerParams(vmem_limit_bytes=40 * 2**20),
+        name="y_stage",
+    )(piece, tab)
+
+
+def z_kernel(in_ref, mix_ref, factor_ref, *rest):
+    out_ref, held = rest[-2:]
+    planes, lines, width = in_ref.shape
+    part = lines // 4
+    for blk in range(lines // 16):
+        cut = slice(blk * 16, (blk + 1) * 16)
+        group = in_ref[:, cut, :].reshape(planes * 16, width)
+        mixed = jnp.dot(mix_ref[...], group, preferred_element_type=F32)
+        held[cut] = mixed.reshape(16, planes, width)
+
+    def body(s, carry):
+        for pair in range(2):
+            left = held[2 * pair * part + s]
+            right = held[(2 * pair + 1) * part + s]
+            lanes = pl.ds(pl.multiple_of((2 * s + pair) * 2 * width, 128), 2 * width)
+            out_ref[0, :, lanes] = jnp.concatenate([left, right], axis=1) * factor_ref[:, lanes]
+        return carry
+
+    lax.fori_loop(0, part, body, 0)
+
+
+def z_stage(comp, piece, mix, factor, before):
+    planes, lines, width = piece.shape
+    whole = lambda a: pl.BlockSpec(a.shape, lambda i: (0,) * a.ndim)
+    args = [piece, mix, factor]
+    specs = [whole(a) for a in args]
+    aliases = {}
+    if before is not None:
+        aliases = {3: 0}
+        args.append(before)
+        specs.append(pl.BlockSpec(memory_space=pl.ANY))
+    return pl.pallas_call(
+        z_kernel,
+        out_shape=jax.ShapeDtypeStruct((3, planes, lines * width), F32),
+        grid=(1,),
+        in_specs=specs,
+        out_specs=pl.BlockSpec((1, planes, lines * width), lambda i: (comp, 0, 0)),
+        scratch_shapes=[pltpu.VMEM((lines, planes, width), F32)],
+        input_output_aliases=aliases,
+        compiler_params=pltpu.CompilerParams(vmem_limit_bytes=40 * 2**20),
+        name="z_stage",
+    )(*args)
+
+
+def coarse_forcing(velocity, eddy_state, eddy_rate, block_owner, block_slot):
+    components, depth, rows, points = velocity.shape
+    coarse_rows = rows // RATIO
+    coarse_cols = points // RATIO
+    xweights = x_weights(points, coarse_cols, RATIO)
+    local = jnp.einsum(
+        "czyn,nx->czyx", velocity, xweights, preferred_element_type=jnp.float32
+    ).astype(jnp.bfloat16)
+    along = padded_2(local, (("row", 2),), 2 * RATIO)
+    yweights = y_weights(coarse_rows, rows + 4 * RATIO, RATIO)
+    filtered = jnp.einsum(
+        "iy,czyx->czix", yweights, along, preferred_element_type=jnp.float32
+    ).astype(jnp.bfloat16)
+    ybands = coarse_rows // BY
+    xbands = coarse_cols // BX
+    count = depth * ybands * xbands
+    blocks = filtered.reshape(components, depth, ybands, BY, xbands, BX).transpose(1, 2, 4, 0, 3, 5)
+    blocks = blocks.reshape(count, BLKV)
+    owners = block_owner.reshape(count)
+    slots = block_slot.reshape(count)
+    owners_total = lax.axis_size("row")
+    every_state, every_rate = (
+        lax.all_gather(eddy_state, "row", axis=1, tiled=True),
+        lax.all_gather(eddy_rate, "row", axis=1, tiled=True),
+    )
+    chosen = owners * S + slots
+    lookup = (chosen[:, None] == jnp.arange(owners_total * S, dtype=jnp.int32)[None, :]).astype(
+        jnp.bfloat16
+    )
+    state = jnp.dot(lookup, every_state[0], preferred_element_type=jnp.float32)
+    rates = jnp.dot(lookup, every_rate[0][:, None], preferred_element_type=jnp.float32)[:, 0]
+    forcing_blocks = (rates[:, None] * (state - blocks.astype(jnp.float32))).astype(jnp.bfloat16)
+    coarse = forcing_blocks.reshape(depth, ybands, xbands, components, BY, BX).transpose(
+        3, 0, 1, 4, 2, 5
+    )
+    return coarse.reshape(components, coarse_rows, coarse_cols)
+
+
+def per_device(velocity, vorticity, eddy_state, eddy_rate, block_owner, block_slot):
+    components, depth, rows, points = velocity.shape
+    n_row, n_col = lax.axis_size("row"), lax.axis_size("col")
+    if depth != 1 or not fits(rows, points, n_row, n_col):
+        return generic_device(velocity, vorticity, eddy_state, eddy_rate, block_owner, block_slot)
+    coarse = coarse_forcing(velocity, eddy_state, eddy_rate, block_owner, block_slot)
+    vel = velocity.reshape(components, rows, points)
+    vort = vorticity.reshape(components, rows, points)
+    xt, xc = (jnp.asarray(t) for t in x_tables_t(points, KXM, n_row))
+    tab = jnp.asarray(y_tables_t(rows * n_row, KYM, rows))
+    planes = depth * n_col
+    inverse = vertical_inverse(planes).astype(jnp.bfloat16)
+    eye = jnp.eye(16, dtype=BF16)
+    mix = (eye[:, None, None, :] * inverse[None, :, :, None]).reshape(16 * planes, planes * 16)
+    mode_rows = KYM // n_col
+    mode_cols = KXM // n_row
+    x_wave = lax.axis_index("row") * mode_cols + jnp.arange(mode_cols, dtype=jnp.int32)
+    y_wave = lax.axis_index("col") * mode_rows + jnp.arange(mode_rows, dtype=jnp.int32) - KYM // 2
+    factor = damping(x_wave, y_wave, NX, NY).reshape(1, -1)
+    result = None
+    spectra = [x_stage(c, vel, vort, coarse, xt, xc, n_row) for c in range(components)]
+    pieces = [lax.all_to_all(s, "row", split_axis=0, concat_axis=0, tiled=True) for s in spectra]
+    ordered = [y_stage(p, tab, n_col) for p in pieces]
+    columns = [lax.all_to_all(o, "col", split_axis=0, concat_axis=0, tiled=True) for o in ordered]
+    for c in range(components):
+        result = z_stage(c, columns[c], mix, factor, result)
+    return result
+
+
 def solution(mesh):
     return jax.shard_map(
         per_device,

time: 589 us -> 224 us (0.38); the launches traced: 582 us -> 223 us
  matrix products: 200 us -> 9.88 us
  local copies, waits for them, and re-layouts: 111 us -> 9.37 us
  other arithmetic: 80.1 us -> 5.95 us
  waiting for transfers between devices: 136 us -> 76 us
  Pallas kernels: 0 us -> 53.1 us
  starting transfers between devices: 15.1 us -> 29.6 us
    dot_general x26 -> x4, matrix products: 200 us -> 9.88 us  [the longest x1 7.99 us: coarse_forcing(): jnp.einsum('czyn,nx->czyx', velocity, xweights, preferred_element_type=jn...]
    all_to_all x2 -> x6, waiting for transfers between devices: 136 us -> 75.9 us  [the longest x3 63.2 us: per_device(): lax.all_to_all(s, 'row', split_axis=0, concat_axis=0, tiled=True)]
    pallas_call x0 -> x9, Pallas kernels: none -> 53.1 us  [the longest x3 29.5 us: x_stage(): pl.pallas_call(lambda *refs: x_kernel(comp, *refs), out_shape=jax.ShapeDt...]
    dot_general x1 -> x0, other arithmetic: 45.1 us -> none  [per_device(): jnp.einsum('kyn,nm->kmy', section.reshape(components * depth, rows, point...]
    broadcast_in_dim x5 -> x0, local copies, waits for them, and re-layouts: 30.2 us -> none  [per_device(): forcing = jnp.repeat(jnp.repeat(coarse, RATIO, axis=2), RATIO, axis=3)]
    convert_element_type x2 -> x1, other arithmetic: 18.9 us -> 0.01 us  [per_device(): eye = jnp.eye(16, dtype=BF16)]
    convert_element_type x5 -> x3, local copies, waits for them, and re-layouts: 18 us -> 0.44 us  [coarse_forcing(): blocks.astype(jnp.float32)]
    all_to_all x2 -> x6, starting transfers between devices: 9.89 us -> 24.4 us  [the longest x3 12.3 us: per_device(): lax.all_to_all(s, 'row', split_axis=0, concat_axis=0, tiled=True)]
  transfers between devices with their start and end apart: 4 -> 8, of which waited for: 2 -> 5; matrix products, arithmetic and copies ran while one was open for 17% -> 4% of each run, Pallas kernels for 0% -> 17%
where the time goes in v1:
time: 224 us; the launch traced here: 223 us
  waiting for transfers between devices  76 us (34%)
  Pallas kernels  53.1 us (24%)
  starting transfers between devices  29.6 us (13%)
  blocking collectives  24.7 us (11%)
  between operations  14.8 us (7%)
  matrix products  9.88 us (4%)
  local copies, waits for them, and re-layouts  9.37 us (4%)
  other arithmetic  5.95 us (3%)
    all_to_all x3, waiting for transfers between devices, per_device(): lax.all_to_all(s, 'row', split_axis=0, concat_axis=0, tiled=True)  63.2 us
    pallas_call x3, Pallas kernels, x_stage(): pl.pallas_call(lambda *refs: x_kernel(comp, *refs), out_shape=jax.ShapeDt...  29.5 us
    pallas_call x3, Pallas kernels, z_stage(): pl.pallas_call(z_kernel, out_shape=jax.ShapeDtypeStruct((3, planes, lines...  16.1 us
    all_gather x1, blocking collectives, coarse_forcing(): lax.all_gather(eddy_state, 'row', axis=1, tiled=True)  14.4 us
    all_to_all x3, waiting for transfers between devices, per_device(): lax.all_to_all(o, 'col', split_axis=0, concat_axis=0, tiled=True)  12.7 us
    all_to_all x3, starting transfers between devices, per_device(): lax.all_to_all(s, 'row', split_axis=0, concat_axis=0, tiled=True)  12.3 us
    all_to_all x3, starting transfers between devices, per_device(): lax.all_to_all(o, 'col', split_axis=0, concat_axis=0, tiled=True)  12.1 us
    reshape x1, blocking collectives  10.3 us
  transfers between devices with their start and end apart: 8, of which 5 were waited for; matrix products, arithmetic and copies ran while one was open for 4% of the time, Pallas kernels for 17%

profile of v1, /device:TPU:0, one launch (start us, length us, event | category | flops | bytes accessed | tf_op | source)
XLA Modules:
  0.0 223.4 jit_solution(15079160168748305569)
XLA Ops:
  0.7 8.0 %fusion.29 = bf16[3,1,512,512]{3,2,0,1:T(8,128)(2,1)S(1)} fusion(f32[]{:T(128)} %fusion.61, s32[512]{0:T(512)S(1)} %iota_multiply_fusion, bf16[3,1,512,2048]{3,2,1,0:T(8,128)(2,1)} %param.9), kind=kOutput, calls=%fused_computation.32 | convolution fusion | flops 3245080576 | bytes 7866372 | tf_op jit(solution)/shard_map/czyn,nx->czyx/dot_general | solution.py:372
  8.7 3.1 %collective-permute-start = (bf16[3,1,8,512]{3,2,0,1:T(8,128)(2,1)S(1)}, bf16[3,1,8,512]{3,2,0,1:T(8,128)(2,1)S(1)}, u32[]{:S(2)}, u32[]{:S(2)}) collective-permute-start(bf16[3,1,8,512]{3,2,0,1:T(8,128)(2,1)S(1)} %get-tuple-element.20), channel_id=1, source_target_pairs={{0,8},{8,16},{16,24},{24,0},{1,9},{9,17},{17,25},{25,1},{2,10},{10... | collective-permute-start | bytes 73736 | tf_op jit(solution)/shard_map/ppermute | solution.py:34
  11.8 2.1 collective-permute-start.1
  15.5 10.3 %all-reduce = bf16[64]{0:T(256)(128)(2,1)S(1)} all-reduce(bf16[64]{0:T(256)(128)(2,1)S(1)} %dynamic-update-slice), channel_id=1, replica_groups=mesh['row'=4,'col'=8] {'row'}, use_global_device_ids=true, to_apply=%add | all-reduce | flops 64 | bytes 256 | tf_op jit(solution)/shard_map/reshape
  25.8 14.4 %all_gather.7 = bf16[1,64,3072]{2,1,0:T(8,128)(2,1)S(1)} all-gather(bf16[1,16,3072]{2,1,0:T(8,128)(2,1)S(1)} %copy-done.6), channel_id=1, replica_groups=mesh['row'=4,'col'=8] {'row'}, dimensions={1}, use_global_device_ids=true | all-gather | bytes 491520 | tf_op jit(solution)/shard_map/all_gather | solution.py:389
  40.4 1.4 fusion.36
  42.7 0.8 copy.19
  43.5 9.8 %x_stage.5 = bf16[4,320,512]{2,1,0:T(8,128)(2,1)} custom-call(bf16[3,512,2048]{2,1,0:T(8,128)(2,1)} %bitcast.90, bf16[3,512,2048]{2,1,0:T(8,128)(2,1)} %bitcast.93, bf16[3,128,512]{2,1,0:T(8,128)(2,1)} %bitcast.96, bf16[1280,2048]{1,0:T(8,128)(2,1)} %constant.83.clone.refs_3_, bf16[1280,512]{1,0:T(8,128)(2,1)} %constant.84.clone.refs_4_), custom_call_target="tpu_custom_call" | custom-call | flops 3355443200 | bytes 20971520 | tf_op jit(solution)/shard_map/x_stage/pallas_call | solution.py:264
  53.3 3.5 %all-to-all-start.4 = ((bf16[4,320,512]{2,1,0:T(8,128)(2,1)}), bf16[4,320,512]{2,1,0:T(8,128)(2,1)S(1)}, u32[]{:S(2)}, u32[]{:S(2)}) async-start(bf16[4,320,512]{2,1,0:T(8,128)(2,1)} %x_stage.5), calls=%async_computation.4 | async-start | bytes 2621440 | tf_op jit(solution)/shard_map/all_to_all | solution.py:426
  56.9 9.9 %x_stage.4 = bf16[4,320,512]{2,1,0:T(8,128)(2,1)} custom-call(bf16[3,512,2048]{2,1,0:T(8,128)(2,1)} %bitcast.91, bf16[3,512,2048]{2,1,0:T(8,128)(2,1)} %bitcast.94, bf16[3,128,512]{2,1,0:T(8,128)(2,1)} %bitcast.97, bf16[1280,2048]{1,0:T(8,128)(2,1)} %constant.83.clone.refs_3_, bf16[1280,512]{1,0:T(8,128)(2,1)} %constant.84.clone.refs_4_), custom_call_target="tpu_custom_call" | custom-call | flops 3355443200 | bytes 20971520 | tf_op jit(solution)/shard_map/x_stage/pallas_call | solution.py:264
  66.7 17.1 %all-to-all-done.4.in_ref = bf16[4,320,512]{2,1,0:T(8,128)(2,1)S(1)} async-done(((bf16[4,320,512]{2,1,0:T(8,128)(2,1)}), bf16[4,320,512]{2,1,0:T(8,128)(2,1)S(1)}, u32[]{:S(2)}, u32[]{:S(2)}) %all-to-all-start.4) | async-done | bytes 1310752 | tf_op jit(solution)/shard_map/all_to_all | solution.py:426
  83.9 4.5 %all-to-all-start.2 = ((bf16[4,320,512]{2,1,0:T(8,128)(2,1)}), bf16[4,320,512]{2,1,0:T(8,128)(2,1)}, u32[]{:S(2)}, u32[]{:S(2)}) async-start(bf16[4,320,512]{2,1,0:T(8,128)(2,1)} %x_stage.4), calls=%async_computation.2 | async-start | bytes 2621440 | tf_op jit(solution)/shard_map/all_to_all | solution.py:426
  88.4 9.8 %x_stage.3 = bf16[4,320,512]{2,1,0:T(8,128)(2,1)} custom-call(bf16[3,512,2048]{2,1,0:T(8,128)(2,1)} %bitcast.92, bf16[3,512,2048]{2,1,0:T(8,128)(2,1)} %bitcast.95, bf16[3,128,512]{2,1,0:T(8,128)(2,1)} %bitcast.98, bf16[1280,2048]{1,0:T(8,128)(2,1)} %constant.83.clone.refs_3_, bf16[1280,512]{1,0:T(8,128)(2,1)} %constant.84.clone.refs_4_), custom_call_target="tpu_custom_call" | custom-call | flops 3355443200 | bytes 20971520 | tf_op jit(solution)/shard_map/x_stage/pallas_call | solution.py:264
  98.2 19.7 %all-to-all-done.2.in_ref = bf16[4,320,512]{2,1,0:T(8,128)(2,1)} async-done(((bf16[4,320,512]{2,1,0:T(8,128)(2,1)}), bf16[4,320,512]{2,1,0:T(8,128)(2,1)}, u32[]{:S(2)}, u32[]{:S(2)}) %all-to-all-start.2) | async-done | bytes 1310752 | tf_op jit(solution)/shard_map/all_to_all | solution.py:426
  117.9 4.3 %all-to-all-start = ((bf16[4,320,512]{2,1,0:T(8,128)(2,1)}), bf16[4,320,512]{2,1,0:T(8,128)(2,1)}, u32[]{:S(2)}, u32[]{:S(2)}) async-start(bf16[4,320,512]{2,1,0:T(8,128)(2,1)} %x_stage.3), calls=%async_computation | async-start | bytes 2621440 | tf_op jit(solution)/shard_map/all_to_all | solution.py:426
  122.9 1.3 copy-done.2
  124.2 1.6 y_stage.5
  125.9 0.9 copy-done.3
  126.8 26.4 %all-to-all-done.in_ref = bf16[4,320,512]{2,1,0:T(8,128)(2,1)} async-done(((bf16[4,320,512]{2,1,0:T(8,128)(2,1)}), bf16[4,320,512]{2,1,0:T(8,128)(2,1)}, u32[]{:S(2)}, u32[]{:S(2)}) %all-to-all-start) | async-done | bytes 1310752 | tf_op jit(solution)/shard_map/all_to_all | solution.py:426
  153.2 4.3 %all-to-all-start.5 = ((bf16[8,160,320]{2,1,0:T(8,128)(2,1)}), bf16[8,160,320]{2,1,0:T(8,128)(2,1)}, u32[]{:S(2)}, u32[]{:S(2)}) async-start(bf16[8,160,320]{2,1,0:T(8,128)(2,1)} %copy-done.3), calls=%async_computation.5 | async-start | bytes 1966080 | tf_op jit(solution)/shard_map/all_to_all | solution.py:428
  172.7 5.1 %fusion.81 = (bf16[1,8]{1,0:T(2,128)(2,1)S(1)}, f32[1,8]{1,0:T(1,128)S(1)}, f32[1,8]{1,0:T(1,128)S(1)}, f32[1,8]{1,0:T(1,128)S(1)}, f32[1,8]{1,0:T(1,128)S(1)}, ...) fusion(f32[]{:T(128)S(6)} %sub.388, f32[]{:T(128)} %bitcast.41, ...), kind=kLoop, calls=%fused_computation.114 | loop fusion | flops 184 | bytes 588 | tf_op jit(solution)/shard_map/convert.11
  177.8 2.9 %y_stage.4 = bf16[8,160,320]{2,1,0:T(8,128)(2,1)S(1)} custom-call(bf16[4,320,512]{2,1,0:T(8,128)(2,1)} %all-to-all-done.2.in_ref, bf16[4,320,1024]{2,1,0:T(8,128)(2,1)S(1)} %copy-done), custom_call_target="tpu_custom_call" | custom-call | flops 838860800 | bytes 10485760 | tf_op jit(solution)/shard_map/y_stage/pallas_call | solution.py:312
  180.7 0.9 copy-done.5
  181.6 4.2 %all-to-all-start.3 = ((bf16[8,160,320]{2,1,0:T(8,128)(2,1)}), bf16[8,160,320]{2,1,0:T(8,128)(2,1)}, u32[]{:S(2)}, u32[]{:S(2)}) async-start(bf16[8,160,320]{2,1,0:T(8,128)(2,1)} %copy-done.5), calls=%async_computation.3 | async-start | bytes 1966080 | tf_op jit(solution)/shard_map/all_to_all | solution.py:428
  185.9 2.9 %y_stage.3 = bf16[8,160,320]{2,1,0:T(8,128)(2,1)S(1)} custom-call(bf16[4,320,512]{2,1,0:T(8,128)(2,1)} %all-to-all-done.in_ref, bf16[4,320,1024]{2,1,0:T(8,128)(2,1)S(1)} %copy-done), custom_call_target="tpu_custom_call" | custom-call | flops 838860800 | bytes 10485760 | tf_op jit(solution)/shard_map/y_stage/pallas_call | solution.py:312
  188.9 1.0 copy-done.4
  189.8 10.8 %all-to-all-done.3.in_ref = bf16[8,160,320]{2,1,0:T(8,128)(2,1)} async-done(((bf16[8,160,320]{2,1,0:T(8,128)(2,1)}), bf16[8,160,320]{2,1,0:T(8,128)(2,1)}, u32[]{:S(2)}, u32[]{:S(2)}) %all-to-all-start.3) | async-done | bytes 819232 | tf_op jit(solution)/shard_map/all_to_all | solution.py:428
  200.6 3.6 %all-to-all-start.1 = ((bf16[8,160,320]{2,1,0:T(8,128)(2,1)}), bf16[8,160,320]{2,1,0:T(8,128)(2,1)S(1)}, u32[]{:S(2)}, u32[]{:S(2)}) async-start(bf16[8,160,320]{2,1,0:T(8,128)(2,1)} %copy-done.4), calls=%async_computation.1 | async-start | bytes 1966080 | tf_op jit(solution)/shard_map/all_to_all | solution.py:428
  205.3 5.8 %z_stage.3.rest_0_ = f32[3,8,51200]{2,1,0:T(8,128)} custom-call(bf16[8,160,320]{2,1,0:T(8,128)(2,1)} %all-to-all-done.5.in_ref, bf16[128,128]{1,0:T(8,128)(2,1)S(1)} %mul.506.mix_ref, f32[1,51200]{1,0:T(1,128)S(1)} %reshape.188.factor_ref), custom_call_target="tpu_custom_call" | custom-call | tf_op jit(solution)/shard_map/z_stage/pallas_call | solution.py:354
  211.1 5.8 %z_stage.4.rest_0_ = f32[3,8,51200]{2,1,0:T(8,128)} custom-call(bf16[8,160,320]{2,1,0:T(8,128)(2,1)} %all-to-all-done.3.in_ref, bf16[128,128]{1,0:T(8,128)(2,1)S(1)} %mul.506.mix_ref, f32[1,51200]{1,0:T(1,128)S(1)} %reshape.188.factor_ref, f32[3,8,51200]{2,1,0:T(8,128)} %z_stage.3.rest_0_), custom_call_target="tpu_custom_call", output_to_operand_aliasing={{}: (3, {})} | custom-call | tf_op jit(solution)/shard_map/z_stage/pallas_call | solution.py:354
  216.9 1.9 all-to-all-done.1.in_ref
  218.8 4.6 %z_stage.5 = f32[3,8,51200]{2,1,0:T(8,128)} custom-call(bf16[8,160,320]{2,1,0:T(8,128)(2,1)S(1)} %all-to-all-done.1.in_ref, bf16[128,128]{1,0:T(8,128)(2,1)S(1)} %mul.506.mix_ref, f32[1,51200]{1,0:T(1,128)S(1)} %reshape.188.factor_ref, f32[3,8,51200]{2,1,0:T(8,128)} %z_stage.4.rest_0_), custom_call_target="tpu_custom_call", output_to_operand_aliasing={{}: (3, {})} | custom-call | tf_op jit(solution)/shard_map/z_stage/pallas_call | solution.py:354
  (54 shorter events, 5.8 us)
Async XLA Ops:
  0.6 13.2 %copy-start.10 = (u32[32]{0:T(128)S(1)}, u32[32]{0:T(128)}, u32[]{:S(2)}) copy-start(u32[32]{0:T(128)} %constant.94) | copy-start | bytes 388
  0.6 14.6 %copy-start.7 = (bf16[1,16]{1,0:T(2,128)(2,1)S(1)}, bf16[1,16]{1,0:T(2,128)(2,1)}, u32[]{:S(2)}) copy-start(bf16[1,16]{1,0:T(2,128)(2,1)} %param.12) | copy-start | bytes 100
  0.6 25.2 %copy-start.6 = (bf16[1,16,3072]{2,1,0:T(8,128)(2,1)S(1)}, bf16[1,16,3072]{2,1,0:T(8,128)(2,1)}, u32[]{:S(2)}) copy-start(bf16[1,16,3072]{2,1,0:T(8,128)(2,1)} %param.11) | copy-start | bytes 294916
  0.6 39.6 %copy-start.8 = (s32[1,1,64]{2,1,0:T(1,128)S(1)}, s32[1,1,64]{2,1,0:T(1,128)}, u32[]{:S(2)}) copy-start(s32[1,1,64]{2,1,0:T(1,128)} %param.14) | copy-start | bytes 772
  0.6 39.6 %copy-start.9 = (s32[1,1,64,1]{2,3,1,0:T(1,128)S(1)}, s32[1,1,64,1]{2,3,1,0:T(1,128)}, u32[]{:S(2)}) copy-start(s32[1,1,64,1]{2,3,1,0:T(1,128)} %param.13) | copy-start | bytes 772
  8.7 31.7 %collective-permute-start = (bf16[3,1,8,512]{3,2,0,1:T(8,128)(2,1)S(1)}, bf16[3,1,8,512]{3,2,0,1:T(8,128)(2,1)S(1)}, u32[]{:S(2)}, u32[]{:S(2)}) collective-permute-start(bf16[3,1,8,512]{3,2,0,1:T(8,128)(2,1)S(1)} %get-tuple-element.20), channel_id=1, source_target_pairs={{0,8},{8,16},{16,24},{24,0},{1,9},{9,17},{17,25},{25,1},{2,10},{10... | collective-permute-start | bytes 73736 | tf_op jit(solution)/shard_map/ppermute | solution.py:34
  11.8 28.7 %collective-permute-start.1 = (bf16[3,1,8,512]{3,2,0,1:T(8,128)(2,1)S(1)}, bf16[3,1,8,512]{3,2,0,1:T(8,128)(2,1)S(1)}, u32[]{:S(2)}, u32[]{:S(2)}) collective-permute-start(bf16[3,1,8,512]{3,2,0,1:T(8,128)(2,1)S(1)} %get-tuple-element.21), channel_id=1, source_target_pairs={{8,0},{16,8},{24,16},{0,24},{9,1},{17,9},{25,17},{1,25},{10,2},{18... | collective-permute-start | bytes 73736 | tf_op jit(solution)/shard_map/ppermute | solution.py:36
  53.3 30.5 %all-to-all-start.4 = ((bf16[4,320,512]{2,1,0:T(8,128)(2,1)}), bf16[4,320,512]{2,1,0:T(8,128)(2,1)S(1)}, u32[]{:S(2)}, u32[]{:S(2)}) async-start(bf16[4,320,512]{2,1,0:T(8,128)(2,1)} %x_stage.5), calls=%async_computation.4 | async-start | bytes 2621440 | tf_op jit(solution)/shard_map/all_to_all | solution.py:426
  83.9 4.5 %copy-start.1 = (bf16[4,320,512]{2,1,0:T(8,128)(2,1)}, bf16[4,320,512]{2,1,0:T(8,128)(2,1)S(1)}, u32[]{:S(2)}) copy-start(bf16[4,320,512]{2,1,0:T(8,128)(2,1)S(1)} %all-to-all-done.4.in_ref) | copy-start | bytes 3932164
  83.9 34.1 %all-to-all-start.2 = ((bf16[4,320,512]{2,1,0:T(8,128)(2,1)}), bf16[4,320,512]{2,1,0:T(8,128)(2,1)}, u32[]{:S(2)}, u32[]{:S(2)}) async-start(bf16[4,320,512]{2,1,0:T(8,128)(2,1)} %x_stage.4), calls=%async_computation.2 | async-start | bytes 2621440 | tf_op jit(solution)/shard_map/all_to_all | solution.py:426
  98.2 24.7 %copy-start = (bf16[4,320,1024]{2,1,0:T(8,128)(2,1)S(1)}, bf16[4,320,1024]{2,1,0:T(8,128)(2,1)}, u32[]{:S(2)}) copy-start(bf16[4,320,1024]{2,1,0:T(8,128)(2,1)} %constant.85.clone.tab_ref) | copy-start | bytes 7864324
  117.9 35.3 %all-to-all-start = ((bf16[4,320,512]{2,1,0:T(8,128)(2,1)}), bf16[4,320,512]{2,1,0:T(8,128)(2,1)}, u32[]{:S(2)}, u32[]{:S(2)}) async-start(bf16[4,320,512]{2,1,0:T(8,128)(2,1)} %x_stage.3), calls=%async_computation | async-start | bytes 2621440 | tf_op jit(solution)/shard_map/all_to_all | solution.py:426
  122.9 1.3 copy-start.2
  125.8 0.9 copy-start.3
  153.2 28.5 %all-to-all-start.5 = ((bf16[8,160,320]{2,1,0:T(8,128)(2,1)}), bf16[8,160,320]{2,1,0:T(8,128)(2,1)}, u32[]{:S(2)}, u32[]{:S(2)}) async-start(bf16[8,160,320]{2,1,0:T(8,128)(2,1)} %copy-done.3), calls=%async_computation.5 | async-start | bytes 1966080 | tf_op jit(solution)/shard_map/all_to_all | solution.py:428
  180.7 0.9 copy-start.5
  181.6 19.0 %all-to-all-start.3 = ((bf16[8,160,320]{2,1,0:T(8,128)(2,1)}), bf16[8,160,320]{2,1,0:T(8,128)(2,1)}, u32[]{:S(2)}, u32[]{:S(2)}) async-start(bf16[8,160,320]{2,1,0:T(8,128)(2,1)} %copy-done.5), calls=%async_computation.3 | async-start | bytes 1966080 | tf_op jit(solution)/shard_map/all_to_all | solution.py:428
  188.8 1.0 copy-start.4
  200.6 18.2 %all-to-all-start.1 = ((bf16[8,160,320]{2,1,0:T(8,128)(2,1)}), bf16[8,160,320]{2,1,0:T(8,128)(2,1)S(1)}, u32[]{:S(2)}, u32[]{:S(2)}) async-start(bf16[8,160,320]{2,1,0:T(8,128)(2,1)} %copy-done.4), calls=%async_computation.1 | async-start | bytes 1966080 | tf_op jit(solution)/shard_map/all_to_all | solution.py:428

commit v2 on v0

--- a/solution.py
+++ b/solution.py
@@ -2,7 +2,10 @@
 
 import jax
 import jax.numpy as jnp
+import numpy as np
 from jax import lax
+from jax.experimental import pallas as pl
+from jax.experimental.pallas import tpu as pltpu
 from jax.sharding import PartitionSpec as P
 
 NX = 2048
@@ -120,7 +123,7 @@
     return jnp.concatenate(outputs, axis=1).astype(jnp.bfloat16)
 
 
-def per_device(velocity, vorticity, eddy_state, eddy_rate, block_owner, block_slot):
+def generic_device(velocity, vorticity, eddy_state, eddy_rate, block_owner, block_slot):
     components, depth, rows, points = velocity.shape
     coarse_rows = rows // RATIO
     coarse_cols = points // RATIO
@@ -190,6 +193,324 @@
     return mixed * factor[None, None, :]
 
 
+MESH = pl.DeviceIdType.MESH
+F32 = jnp.float32
+BF16 = jnp.bfloat16
+YB = 256
+NT = (((1,), (1,)), ((), ()))
+
+
+def fits(rows, points, n_row, n_col):
+    mode_cols, mode_rows = KXM // n_row, KYM // n_col
+    return (
+        n_row == 4
+        and rows % YB == 0
+        and points % 512 == 0
+        and mode_cols % 16 == 0
+        and (2 * mode_cols) % 128 == 64
+        and mode_rows % 32 == 0
+        and n_col == 8
+    )
+
+
+def x_tables_t(points, kept, n_row):
+    per = kept // n_row
+    row = np.arange(2 * kept)
+    wave = row // (2 * per) * per + row % per
+    imag = row // per % 2
+    phase = (wave[:, None] * np.arange(points)[None, :]) % points * (2.0 * math.pi / points)
+    value = np.where(imag[:, None] == 0, np.cos(phase), -np.sin(phase)) / math.sqrt(points)
+    fine = value.astype(BF16)
+    coarse = section_step * fine.astype(np.float32).reshape(2 * kept, points // RATIO, RATIO).sum(2)
+    return fine, coarse.astype(BF16)
+
+
+def y_tables_t(points, kept, quarter):
+    s = np.arange(kept // 4)
+    out = []
+    for q in range(4):
+        wave = 4 * s + q - kept // 2
+        phase = (wave[:, None] * np.arange(quarter)[None, :]) % points * (2.0 * math.pi / points)
+        out.append(np.concatenate([np.cos(phase), np.sin(phase)], axis=1) / math.sqrt(points))
+    return np.stack(out).astype(BF16)
+
+
+def all_kernel(
+    vel, vort, coarse, xt, xc, tab, mix, out,
+    velv, vortv, coarsev, xtv, xcv, tabv, section, repeated, xsend, xrecv, ysend, yrecv, held, done,
+    load_sem, xs_sem, xr_sem, ys_sem, yr_sem, out_sem,
+):
+    me, mc = lax.axis_index("row"), lax.axis_index("col")
+    n_row, n_col = 4, yrecv.shape[1]
+    _, rows, points = velv.shape
+    width = xsend.shape[2]
+    barrier = pltpu.get_barrier_semaphore()
+    for d in range(1, n_row):
+        pl.semaphore_signal(
+            barrier, inc=1, device_id={"row": lax.rem(me + d, n_row)}, device_id_type=MESH
+        )
+    for d in range(1, n_col):
+        pl.semaphore_signal(
+            barrier, inc=1, device_id={"col": lax.rem(mc + d, n_col)}, device_id_type=MESH
+        )
+    loads = []
+    for src, dst in (
+        (vel, velv), (vort, vortv), (coarse, coarsev), (xt, xtv), (xc, xcv), (tab, tabv),
+    ):
+        loads.append(pltpu.make_async_copy(src, dst, load_sem.at[len(loads)]))
+        loads[-1].start()
+    for load in loads[:3]:
+        load.wait()
+    pl.semaphore_wait(barrier, n_row + n_col - 2)
+
+    far = me // 2
+    order = [3 * (1 - far), 2 - far, 1 + 4 * far - me, me]
+    fine = lax.broadcasted_iota(jnp.int32, (rows, rows // RATIO), 0) // RATIO
+    cell = lax.broadcasted_iota(jnp.int32, (rows, rows // RATIO), 1)
+    spread = jnp.where(fine == cell, 1.0, 0.0).astype(BF16)
+
+    def xcopy(comp, k, dest):
+        return pltpu.make_async_remote_copy(
+            src_ref=xsend.at[comp, k],
+            dst_ref=xrecv.at[comp, me],
+            send_sem=xs_sem.at[comp, k],
+            recv_sem=xr_sem.at[comp, me],
+            device_id={"row": dest},
+            device_id_type=MESH,
+        )
+
+    def xbody(comp, carry):
+        b, c = lax.rem(comp + 1, 3), lax.rem(comp + 2, 3)
+
+        def piece(i, inner):
+            lines = pl.ds(pl.multiple_of(i * 16, 16), 16)
+            cross = velv[b, lines, :].astype(F32) * vortv[c, lines, :].astype(F32)
+            cross = cross - velv[c, lines, :].astype(F32) * vortv[b, lines, :].astype(F32)
+            section[lines, :] = (velv[comp, lines, :].astype(F32) + section_step * cross).astype(BF16)
+            return inner
+
+        lax.fori_loop(0, rows // 16, piece, 0)
+        repeated[...] = jnp.dot(spread, coarsev[comp], preferred_element_type=F32).astype(BF16)
+
+        @pl.when(comp == 0)
+        def _():
+            loads[3].wait()
+            loads[4].wait()
+
+        for k in range(n_row):
+            lines = pl.ds(pl.multiple_of(order[k] * width, 16), width)
+            total = lax.dot_general(xtv[lines, :], section[...], NT, preferred_element_type=F32)
+            total += lax.dot_general(xcv[lines, :], repeated[...], NT, preferred_element_type=F32)
+            if k < n_row - 1:
+                xsend[comp, k] = total.astype(BF16)
+                xcopy(comp, k, order[k]).start()
+            else:
+                xrecv[comp, me] = total.astype(BF16)
+        return carry
+
+    lax.fori_loop(0, 3, xbody, 0)
+    loads[5].wait()
+
+    def ycopy(comp, d):
+        dest = lax.rem(mc + d, n_col)
+        return pltpu.make_async_remote_copy(
+            src_ref=ysend.at[comp, dest],
+            dst_ref=yrecv.at[comp, mc],
+            send_sem=ys_sem.at[comp, d - 1],
+            recv_sem=yr_sem.at[comp, mc],
+            device_id={"col": dest},
+            device_id_type=MESH,
+        )
+
+    def ystage(comp):
+        for d in range(1, n_row):
+            source = lax.rem(me + d, n_row)
+            pltpu.make_async_remote_copy(
+                src_ref=xsend.at[comp, 0],
+                dst_ref=xrecv.at[comp, source],
+                send_sem=xs_sem.at[comp, 0],
+                recv_sem=xr_sem.at[comp, source],
+                device_id={"row": source},
+                device_id_type=MESH,
+            ).wait_recv()
+        half = width // 2
+        a = [xrecv[comp, r, :half, :].astype(F32) for r in range(4)]
+        b = [xrecv[comp, r, half:, :].astype(F32) for r in range(4)]
+        a02, a13, b02, b13 = a[0] + a[2], a[1] + a[3], b[0] + b[2], b[1] + b[3]
+        d02, d13, e02, e13 = a[0] - a[2], a[1] - a[3], b[0] - b[2], b[1] - b[3]
+        real = [a02 + a13, d02 + e13, a02 - a13, d02 - e13]
+        imag = [b02 + b13, e02 - d13, b02 - b13, e02 + d13]
+        results = []
+        for q in range(4):
+            re, im = real[q].astype(BF16), imag[q].astype(BF16)
+            turned = jnp.concatenate(
+                [jnp.concatenate([re, im], axis=0), jnp.concatenate([im, -re], axis=0)], axis=1
+            )
+            results.append(lax.dot_general(tabv[q], turned, NT, preferred_element_type=F32))
+        part = ysend.shape[2] // 4
+        for d in range(n_col):
+            ysend[comp, d] = jnp.concatenate(
+                [results[q][d * part : (d + 1) * part] for q in range(4)], axis=0
+            ).astype(BF16)
+        for d in range(1, n_col):
+            ycopy(comp, d).start()
+        yrecv[comp, mc] = ysend[comp, mc]
+
+    def zstage(comp):
+        for d in range(1, n_col):
+            source = lax.rem(mc + d, n_col)
+            pltpu.make_async_remote_copy(
+                src_ref=ysend.at[comp, source],
+                dst_ref=yrecv.at[comp, source],
+                send_sem=ys_sem.at[comp, d - 1],
+                recv_sem=yr_sem.at[comp, source],
+                device_id={"col": source},
+                device_id_type=MESH,
+            ).wait_recv()
+        lines, planes, _ = held.shape
+        part = lines // 4
+        for blk in range(lines // 16):
+            cut = slice(blk * 16, (blk + 1) * 16)
+            group = yrecv[comp, :, cut, :].reshape(planes * 16, width)
+            mixed = jnp.dot(mix[...], group, preferred_element_type=F32)
+            held[cut] = mixed.reshape(16, planes, width)
+
+        def body(s, carry):
+            for pair in range(2):
+                left = held[2 * pair * part + s]
+                right = held[(2 * pair + 1) * part + s]
+                lanes = pl.ds(pl.multiple_of((2 * s + pair) * 2 * width, 128), 2 * width)
+                done[comp, :, lanes] = jnp.concatenate([left, right], axis=1)
+            return carry
+
+        lax.fori_loop(0, part, body, 0, unroll=4)
+        pltpu.make_async_copy(done.at[comp], out.at[comp], out_sem.at[comp]).start()
+
+    ystage(0)
+    ystage(1)
+    zstage(0)
+    ystage(2)
+    zstage(1)
+    zstage(2)
+    for comp in range(3):
+        pltpu.make_async_copy(done.at[comp], out.at[comp], out_sem.at[comp]).wait()
+        for k in range(n_row - 1):
+            xcopy(comp, k, order[k]).wait_send()
+        for d in range(1, n_col):
+            ycopy(comp, d).wait_send()
+
+
+def all_stages(vel, vort, coarse, xt, xc, tab, mix, n_row, n_col):
+    _, rows, points = vel.shape
+    width = xt.shape[0] // n_row
+    lines = 4 * tab.shape[1] // n_col
+    anywhere = pl.BlockSpec(memory_space=pl.ANY)
+    dma = pltpu.SemaphoreType.DMA
+    return pl.pallas_call(
+        all_kernel,
+        out_shape=jax.ShapeDtypeStruct((3, n_col, lines * width), F32),
+        in_specs=[anywhere] * 6 + [pl.BlockSpec(memory_space=pltpu.VMEM)],
+        out_specs=anywhere,
+        scratch_shapes=[
+            pltpu.VMEM(vel.shape, BF16),
+            pltpu.VMEM(vort.shape, BF16),
+            pltpu.VMEM(coarse.shape, BF16),
+            pltpu.VMEM(xt.shape, BF16),
+            pltpu.VMEM(xc.shape, BF16),
+            pltpu.VMEM(tab.shape, BF16),
+            pltpu.VMEM((rows, points), BF16),
+            pltpu.VMEM((rows, points // RATIO), BF16),
+            pltpu.VMEM((3, n_row, width, rows), BF16),
+            pltpu.VMEM((3, n_row, width, rows), BF16),
+            pltpu.VMEM((3, n_col, lines, width), BF16),
+            pltpu.VMEM((3, n_col, lines, width), BF16),
+            pltpu.VMEM((lines, n_col, width), F32),
+            pltpu.VMEM((3, n_col, lines * width), F32),
+            dma((6,)),
+            dma((3, n_row)),
+            dma((3, n_row)),
+            dma((3, n_col)),
+            dma((3, n_col)),
+            dma((3,)),
+        ],
+        compiler_params=pltpu.CompilerParams(
+            collective_id=0, has_side_effects=True, vmem_limit_bytes=60 * 2**20
+        ),
+        name="all_stages",
+    )(vel, vort, coarse, xt, xc, tab, mix)
+
+
+def coarse_forcing(velocity, eddy_state, eddy_rate, block_owner, block_slot):
+    components, depth, rows, points = velocity.shape
+    coarse_rows = rows // RATIO
+    coarse_cols = points // RATIO
+    xweights = x_weights(points, coarse_cols, RATIO)
+    local = jnp.einsum(
+        "czyn,nx->czyx", velocity, xweights, preferred_element_type=jnp.float32
+    ).astype(jnp.bfloat16)
+    along = padded_2(local, (("row", 2),), 2 * RATIO)
+    yweights = y_weights(coarse_rows, rows + 4 * RATIO, RATIO)
+    filtered = jnp.einsum(
+        "iy,czyx->czix", yweights, along, preferred_element_type=jnp.float32
+    ).astype(jnp.bfloat16)
+    ybands = coarse_rows // BY
+    xbands = coarse_cols // BX
+    count = depth * ybands * xbands
+    blocks = filtered.reshape(components, depth, ybands, BY, xbands, BX).transpose(1, 2, 4, 0, 3, 5)
+    blocks = blocks.reshape(count, BLKV)
+    owners = block_owner.reshape(count)
+    slots = block_slot.reshape(count)
+    owners_total = lax.axis_size("row")
+    every_state, every_rate = (
+        lax.all_gather(eddy_state, "row", axis=1, tiled=True),
+        lax.all_gather(eddy_rate, "row", axis=1, tiled=True),
+    )
+    chosen = owners * S + slots
+    lookup = (chosen[:, None] == jnp.arange(owners_total * S, dtype=jnp.int32)[None, :]).astype(
+        jnp.bfloat16
+    )
+    state = jnp.dot(lookup, every_state[0], preferred_element_type=jnp.float32)
+    rates = jnp.dot(lookup, every_rate[0][:, None], preferred_element_type=jnp.float32)[:, 0]
+    forcing_blocks = (rates[:, None] * (state - blocks.astype(jnp.float32))).astype(jnp.bfloat16)
+    coarse = forcing_blocks.reshape(depth, ybands, xbands, components, BY, BX).transpose(
+        3, 0, 1, 4, 2, 5
+    )
+    return coarse.reshape(components, coarse_rows, coarse_cols)
+
+
+def vertical_inverse_np(planes):
+    index = np.arange(planes)
+    ends = (index == 0) | (index == planes - 1)
+    matrix = np.diag(np.where(ends, 1.0 + vertical_step, 1.0 + 2.0 * vertical_step))
+    for i in range(planes - 1):
+        matrix[i, i + 1] = matrix[i + 1, i] = -vertical_step
+    return np.linalg.inv(matrix).astype(np.float32)
+
+
+def per_device(velocity, vorticity, eddy_state, eddy_rate, block_owner, block_slot):
+    components, depth, rows, points = velocity.shape
+    n_row, n_col = lax.axis_size("row"), lax.axis_size("col")
+    if depth != 1 or not fits(rows, points, n_row, n_col):
+        return generic_device(velocity, vorticity, eddy_state, eddy_rate, block_owner, block_slot)
+    coarse = coarse_forcing(velocity, eddy_state, eddy_rate, block_owner, block_slot)
+    vel = velocity.reshape(components, rows, points)
+    vort = vorticity.reshape(components, rows, points)
+    xt, xc = (jnp.asarray(t) for t in x_tables_t(points, KXM, n_row))
+    tab = jnp.asarray(y_tables_t(rows * n_row, KYM, rows))
+    mix = jnp.asarray(
+        np.einsum("vz,ts->tvzs", vertical_inverse_np(n_col), np.eye(16))
+        .reshape(16 * n_col, n_col * 16)
+        .astype(BF16)
+    )
+    mode_rows = KYM // n_col
+    mode_cols = KXM // n_row
+    x_wave = lax.axis_index("row") * mode_cols + jnp.arange(mode_cols, dtype=jnp.int32)
+    y_wave = lax.axis_index("col") * mode_rows + jnp.arange(mode_rows, dtype=jnp.int32) - KYM // 2
+    factor = damping(x_wave, y_wave, NX, NY).reshape(-1)
+    mixed = all_stages(vel, vort, coarse, xt, xc, tab, mix, n_row, n_col)
+    return mixed * factor[None, None, :]
+
+
 def solution(mesh):
     return jax.shard_map(
         per_device,

time: 589 us -> 157 us (0.27)
  the two profiles are of different devices: /device:TPU:0 before, /device:TPU:9 now
where the time goes in v2:
time: 157 us
  Pallas kernels  116 us (74%)
  blocking collectives  18.9 us (12%)
  matrix products  11.2 us (7%)
  other arithmetic  5.77 us (4%)
  local copies, waits for them, and re-layouts  2.7 us (2%)
    pallas_call x1, Pallas kernels, all_stages(): pl.pallas_call(all_kernel, out_shape=jax.ShapeDtypeStruct((3, n_col, line...  116 us
    all_gather x1, blocking collectives, coarse_forcing(): lax.all_gather(eddy_state, 'row', axis=1, tiled=True)  10.3 us
    reshape x1, blocking collectives  8.63 us
    dot_general x1, matrix products, coarse_forcing(): jnp.einsum('czyn,nx->czyx', velocity, xweights, preferred_element_type=jn...  7.97 us
    mul x1, other arithmetic, per_device(): return mixed * factor[None, None, :]  5.01 us
  transfers between devices with their start and end apart: 2, of which 0 were waited for; matrix products, arithmetic and copies ran while one was open for 1% of the time, Pallas kernels for 0%

profile of v2, /device:TPU:9, one launch (start us, length us, event | category | flops | bytes accessed | tf_op | source)
XLA Modules:
  0.0 156.8 jit_solution(16022664265244286801)
XLA Ops:
  0.0 0.6 fusion.59
  0.6 0.0 copy-start.3
  0.6 0.0 copy-start.4
  0.7 8.0 %fusion.29 = bf16[3,1,512,512]{3,2,0,1:T(8,128)(2,1)S(1)} fusion(f32[]{:T(128)} %fusion.59, s32[512]{0:T(512)S(1)} %iota_multiply_fusion, bf16[3,1,512,2048]{3,2,1,0:T(8,128)(2,1)} %param.10), kind=kOutput, calls=%fused_computation.33 | convolution fusion | flops 3245080576 | bytes 7866372 | tf_op jit(solution)/shard_map/czyn,nx->czyx/dot_general | solution.py:448
  8.6 0.0 copy-start.1
  8.7 1.3 collective-permute-start
  10.0 0.2 collective-permute-start.1
  10.2 0.0 copy-done.1
  10.2 0.0 copy-done.5
  10.2 0.6 dynamic-slice
  11.3 0.0 copy-done.2
  11.3 0.2 dynamic-update-slice
  11.6 8.6 %all-reduce = bf16[64]{0:T(256)(128)(2,1)S(1)} all-reduce(bf16[64]{0:T(256)(128)(2,1)S(1)} %dynamic-update-slice), channel_id=1, replica_groups=mesh['row'=4,'col'=8] {'row'}, use_global_device_ids=true, to_apply=%add | all-reduce | flops 64 | bytes 256 | tf_op jit(solution)/shard_map/reshape
  20.2 0.0 copy-done
  20.2 10.3 %all_gather.7 = bf16[1,64,3072]{2,1,0:T(8,128)(2,1)S(1)} all-gather(bf16[1,16,3072]{2,1,0:T(8,128)(2,1)S(1)} %copy-done), channel_id=1, replica_groups=mesh['row'=4,'col'=8] {'row'}, dimensions={1}, use_global_device_ids=true | all-gather | bytes 491520 | tf_op jit(solution)/shard_map/all_gather | solution.py:465
  30.5 0.0 copy-done.3
  30.5 0.0 copy-done.4
  30.5 0.2 convolution_bitcast_fusion
  30.7 0.1 multiply_exponential_fusion
  30.8 0.1 broadcast_in_dim.12
  30.9 0.4 mul.134
  31.4 0.0 collective-permute-done
  31.4 0.0 collective-permute-done.1
  31.4 2.8 %fusion.36 = f32[3,1,128,512]{2,3,0,1:T(8,128)S(1)} fusion(bf16[3,1,8,512]{3,2,0,1:T(8,128)(2,1)S(1)} %collective-permute-done.1, bf16[3,1,512,512]{3,2,0,1:T(8,128)(2,1)} %copy-done.1, bf16[3,1,8,512]{3,2,0,1:T(8,128)(2,1)S(1)} %collective-permute-done, f32[]{:T(128)} %fusion.59, s32[128]{0:T(128)S(1)} %iota_multiply_fusion.1), kind=kOutput, calls=%fused_computation.38 | convolution fusion | flops 213688320 | bytes 2408964 | tf_op jit(solution)/shard_map/iy,czyx->czix/dot_general | solution.py:453
  34.2 0.3 copy.13
  34.4 0.1 copy.14
  34.5 0.1 reshape.117
  34.6 0.3 fusion.33
  34.9 0.1 copy.16
  35.0 0.8 copy.18
  35.8 116.0 %all_stages.1 = f32[3,8,51200]{2,1,0:T(8,128)} custom-call(bf16[3,512,2048]{2,1,0:T(8,128)(2,1)} %bitcast.66, bf16[3,512,2048]{2,1,0:T(8,128)(2,1)} %bitcast.67, bf16[3,128,512]{2,1,0:T(8,128)(2,1)} %bitcast.70, bf16[1280,2048]{1,0:T(8,128)(2,1)} %constant.76.clone.xt, bf16[1280,512]{1,0:T(8,128)(2,1)} %constant.77.clone.xc, ...), custom_call_target="tpu_custom_call" | custom-call | tf_op jit(solution)/shard_map/all_stages/pallas_call | solution.py:409
  151.8 5.0 %broadcast_multiply_fusion = f32[3,8,51200]{2,1,0:T(8,128)} fusion(f32[3,8,51200]{2,1,0:T(8,128)} %all_stages.1, f32[51200]{0:T(1024)S(1)} %mul.134), kind=kLoop, calls=%fused_computation.13 | loop fusion | flops 1228800 | bytes 10035200 | tf_op jit(solution)/shard_map/mul | solution.py:511
  (9 shorter events, 0.0 us)
Async XLA Ops:
  0.6 9.6 %copy-start.5 = (u32[32]{0:T(128)S(1)}, u32[32]{0:T(128)}, u32[]{:S(2)}) copy-start(u32[32]{0:T(128)} %constant.88) | copy-start | bytes 388
  0.6 10.7 %copy-start.2 = (bf16[1,16]{1,0:T(2,128)(2,1)S(1)}, bf16[1,16]{1,0:T(2,128)(2,1)}, u32[]{:S(2)}) copy-start(bf16[1,16]{1,0:T(2,128)(2,1)} %param.13) | copy-start | bytes 100
  0.6 19.6 %copy-start = (bf16[1,16,3072]{2,1,0:T(8,128)(2,1)S(1)}, bf16[1,16,3072]{2,1,0:T(8,128)(2,1)}, u32[]{:S(2)}) copy-start(bf16[1,16,3072]{2,1,0:T(8,128)(2,1)} %param.12) | copy-start | bytes 294916
  0.6 29.8 %copy-start.3 = (s32[1,1,64]{2,1,0:T(1,128)S(1)}, s32[1,1,64]{2,1,0:T(1,128)}, u32[]{:S(2)}) copy-start(s32[1,1,64]{2,1,0:T(1,128)} %param.15) | copy-start | bytes 772
  0.6 29.8 %copy-start.4 = (s32[1,1,64,1]{2,3,1,0:T(1,128)S(1)}, s32[1,1,64,1]{2,3,1,0:T(1,128)}, u32[]{:S(2)}) copy-start(s32[1,1,64,1]{2,3,1,0:T(1,128)} %param.14) | copy-start | bytes 772
  8.6 1.5 copy-start.1
  8.7 22.7 %collective-permute-start = (bf16[3,1,8,512]{3,2,0,1:T(8,128)(2,1)S(1)}, bf16[3,1,8,512]{3,2,0,1:T(8,128)(2,1)S(1)}, u32[]{:S(2)}, u32[]{:S(2)}) collective-permute-start(bf16[3,1,8,512]{3,2,0,1:T(8,128)(2,1)S(1)} %get-tuple-element.5), channel_id=1, source_target_pairs={{0,8},{8,16},{16,24},{24,0},{1,9},{9,17},{17,25},{25,1},{2,10},{10... | collective-permute-start | bytes 73736 | tf_op jit(solution)/shard_map/ppermute | solution.py:34
  10.0 21.4 %collective-permute-start.1 = (bf16[3,1,8,512]{3,2,0,1:T(8,128)(2,1)S(1)}, bf16[3,1,8,512]{3,2,0,1:T(8,128)(2,1)S(1)}, u32[]{:S(2)}, u32[]{:S(2)}) collective-permute-start(bf16[3,1,8,512]{3,2,0,1:T(8,128)(2,1)S(1)} %get-tuple-element.6), channel_id=1, source_target_pairs={{8,0},{16,8},{24,16},{0,24},{9,1},{17,9},{25,17},{1,25},{10,2},{18... | collective-permute-start | bytes 73736 | tf_op jit(solution)/shard_map/ppermute | solution.py:36

commit v3 on v2

--- a/solution.py
+++ b/solution.py
@@ -205,7 +205,8 @@
     return (
         n_row == 4
         and rows % YB == 0
-        and points % 512 == 0
+        and points % 1024 == 0
+        and points >= 2048
         and mode_cols % 16 == 0
         and (2 * mode_cols) % 128 == 64
         and mode_rows % 32 == 0
@@ -236,9 +237,9 @@
 
 
 def all_kernel(
-    vel, vort, coarse, xt, xc, tab, mix, out,
-    velv, vortv, coarsev, xtv, xcv, tabv, section, repeated, xsend, xrecv, ysend, yrecv, held, done,
-    load_sem, xs_sem, xr_sem, ys_sem, yr_sem, out_sem,
+    vel, vort, xt, xc, tab, mix, state, chosen, xw, yw, ytop, ybot, out,
+    velv, vortv, coarsev, along, edges, every, xtv, xcv, tabv, section, repeated, xsend, xrecv, ysend, yrecv, held, done,
+    load_sem, es_sem, er_sem, ss_sem, sr_sem, xs_sem, xr_sem, ys_sem, yr_sem, out_sem,
 ):
     me, mc = lax.axis_index("row"), lax.axis_index("col")
     n_row, n_col = 4, yrecv.shape[1]
@@ -255,13 +256,102 @@
         )
     loads = []
     for src, dst in (
-        (vel, velv), (vort, vortv), (coarse, coarsev), (xt, xtv), (xc, xcv), (tab, tabv),
+        (vel, velv), (vort, vortv), (xt, xtv), (xc, xcv), (tab, tabv),
     ):
         loads.append(pltpu.make_async_copy(src, dst, load_sem.at[len(loads)]))
         loads[-1].start()
-    for load in loads[:3]:
-        load.wait()
     pl.semaphore_wait(barrier, n_row + n_col - 2)
+
+    def scopy(d):
+        return pltpu.make_async_remote_copy(
+            src_ref=state,
+            dst_ref=every.at[:, me],
+            send_sem=ss_sem.at[d - 1],
+            recv_sem=sr_sem.at[me],
+            device_id={"row": lax.rem(me + d, n_row)},
+            device_id_type=MESH,
+        )
+
+    def ecopy(side):
+        dest = lax.rem(me + (1 if side == 0 else n_row - 1), n_row)
+        lines = slice(rows - 16, rows) if side == 0 else slice(0, 16)
+        return pltpu.make_async_remote_copy(
+            src_ref=along.at[:, lines, :],
+            dst_ref=edges.at[side],
+            send_sem=es_sem.at[side],
+            recv_sem=er_sem.at[side],
+            device_id={"row": dest},
+            device_id_type=MESH,
+        )
+
+    for d in range(1, n_row):
+        scopy(d).start()
+    loads[0].wait()
+    cells = points // RATIO
+
+    def filter_x(comp, carry):
+        for h in range(cells // 256):
+            low, high = 256 * RATIO * h - 128, 256 * RATIO * h + 256 * RATIO + 128
+            cuts = [(max(low, 0), min(high, points), max(-low, 0))]
+            if low < 0:
+                cuts.append((points + low, points, 0))
+            if high > points:
+                cuts.append((0, high - points, points - low))
+            total = 0.0
+            for start, stop, at in cuts:
+                total += jnp.dot(
+                    velv[comp, :, start:stop],
+                    xw[at : at + stop - start, :],
+                    preferred_element_type=F32,
+                )
+            along[comp, :, 256 * h : 256 * (h + 1)] = total.astype(BF16)
+        return carry
+
+    lax.fori_loop(0, 3, filter_x, 0)
+    ecopy(0).start()
+    ecopy(1).start()
+    every[:, me] = state[...]
+    for d in range(1, n_row):
+        source = lax.rem(me + d, n_row)
+        pltpu.make_async_remote_copy(
+            src_ref=state,
+            dst_ref=every.at[:, source],
+            send_sem=ss_sem.at[d - 1],
+            recv_sem=sr_sem.at[source],
+            device_id={"row": source},
+            device_id_type=MESH,
+        ).wait_recv()
+    ecopy(0).wait_recv()
+    ecopy(1).wait_recv()
+    slots = every.shape[1] * every.shape[2]
+    lows = rows // RATIO
+    sides = xw.shape[1] // 2
+    smooth = []
+    for comp in range(3):
+        total = jnp.dot(yw[...], along[comp], preferred_element_type=F32)
+        total += jnp.dot(ytop[...], edges[0, comp], preferred_element_type=F32)
+        total += jnp.dot(ybot[...], edges[1, comp], preferred_element_type=F32)
+        smooth.append(total.astype(BF16).astype(F32))
+    deep = lax.broadcasted_iota(jnp.int32, (lows, BY * slots), 1)
+    inner = (lax.broadcasted_iota(jnp.int32, (lows, BY * slots), 0) & (BY - 1)) * slots
+    flat = lax.broadcasted_iota(jnp.int32, (lows, slots), 1)
+    for q in range(cells // BX):
+        name = chosen[:, q : q + 1]
+        pick = jnp.where(deep == inner + name, 1.0, 0.0).astype(BF16)
+        rate = jnp.dot(
+            jnp.where(flat == name, 1.0, 0.0).astype(BF16),
+            every[3 * BY].reshape(slots, BX),
+            preferred_element_type=F32,
+        )
+        for comp in range(3):
+            held_state = jnp.dot(
+                pick,
+                every[comp * BY : (comp + 1) * BY].reshape(BY * slots, BX),
+                preferred_element_type=F32,
+            )
+            lanes = slice(q * BX, (q + 1) * BX)
+            coarsev[comp, :, lanes] = (rate * (held_state - smooth[comp][:, lanes])).astype(BF16)
+    loads[1].wait()
 
     far = me // 2
     order = [3 * (1 - far), 2 - far, 1 + 4 * far - me, me]
@@ -294,8 +384,8 @@
 
         @pl.when(comp == 0)
         def _():
+            loads[2].wait()
             loads[3].wait()
-            loads[4].wait()
 
         for k in range(n_row):
             lines = pl.ds(pl.multiple_of(order[k] * width, 16), width)
@@ -309,7 +399,7 @@
         return carry
 
     lax.fori_loop(0, 3, xbody, 0)
-    loads[5].wait()
+    loads[4].wait()
 
     def ycopy(comp, d):
         dest = lax.rem(mc + d, n_col)
@@ -392,6 +482,10 @@
     ystage(2)
     zstage(1)
     zstage(2)
+    for d in range(1, n_row):
+        scopy(d).wait_send()
+    ecopy(0).wait_send()
+    ecopy(1).wait_send()
     for comp in range(3):
         pltpu.make_async_copy(done.at[comp], out.at[comp], out_sem.at[comp]).wait()
         for k in range(n_row - 1):
@@ -400,8 +494,10 @@
             ycopy(comp, d).wait_send()
 
 
-def all_stages(vel, vort, coarse, xt, xc, tab, mix, n_row, n_col):
+def all_stages(vel, vort, xt, xc, tab, mix, small, n_row, n_col):
     _, rows, points = vel.shape
+    cells = points // RATIO
+    state = small[0].shape
     width = xt.shape[0] // n_row
     lines = 4 * tab.shape[1] // n_col
     anywhere = pl.BlockSpec(memory_space=pl.ANY)
@@ -409,12 +505,15 @@
     return pl.pallas_call(
         all_kernel,
         out_shape=jax.ShapeDtypeStruct((3, n_col, lines * width), F32),
-        in_specs=[anywhere] * 6 + [pl.BlockSpec(memory_space=pltpu.VMEM)],
+        in_specs=[anywhere] * 5 + [pl.BlockSpec(memory_space=pltpu.VMEM)] * (1 + len(small)),
         out_specs=anywhere,
         scratch_shapes=[
             pltpu.VMEM(vel.shape, BF16),
             pltpu.VMEM(vort.shape, BF16),
-            pltpu.VMEM(coarse.shape, BF16),
+            pltpu.VMEM((3, rows // RATIO, cells), BF16),
+            pltpu.VMEM((3, rows, cells), BF16),
+            pltpu.VMEM((2, 3, 16, cells), BF16),
+            pltpu.VMEM((state[0], n_row, state[1], state[2]), BF16),
             pltpu.VMEM(xt.shape, BF16),
             pltpu.VMEM(xc.shape, BF16),
             pltpu.VMEM(tab.shape, BF16),
@@ -426,7 +525,11 @@
             pltpu.VMEM((3, n_col, lines, width), BF16),
             pltpu.VMEM((lines, n_col, width), F32),
             pltpu.VMEM((3, n_col, lines * width), F32),
-            dma((6,)),
+            dma((5,)),
+            dma((2,)),
+            dma((2,)),
+            dma((n_row,)),
+            dma((n_row,)),
             dma((3, n_row)),
             dma((3, n_row)),
             dma((3, n_col)),
@@ -437,45 +540,24 @@
             collective_id=0, has_side_effects=True, vmem_limit_bytes=60 * 2**20
         ),
         name="all_stages",
-    )(vel, vort, coarse, xt, xc, tab, mix)
-
-
-def coarse_forcing(velocity, eddy_state, eddy_rate, block_owner, block_slot):
-    components, depth, rows, points = velocity.shape
-    coarse_rows = rows // RATIO
-    coarse_cols = points // RATIO
-    xweights = x_weights(points, coarse_cols, RATIO)
-    local = jnp.einsum(
-        "czyn,nx->czyx", velocity, xweights, preferred_element_type=jnp.float32
-    ).astype(jnp.bfloat16)
-    along = padded_2(local, (("row", 2),), 2 * RATIO)
-    yweights = y_weights(coarse_rows, rows + 4 * RATIO, RATIO)
-    filtered = jnp.einsum(
-        "iy,czyx->czix", yweights, along, preferred_element_type=jnp.float32
-    ).astype(jnp.bfloat16)
-    ybands = coarse_rows // BY
-    xbands = coarse_cols // BX
-    count = depth * ybands * xbands
-    blocks = filtered.reshape(components, depth, ybands, BY, xbands, BX).transpose(1, 2, 4, 0, 3, 5)
-    blocks = blocks.reshape(count, BLKV)
-    owners = block_owner.reshape(count)
-    slots = block_slot.reshape(count)
-    owners_total = lax.axis_size("row")
-    every_state, every_rate = (
-        lax.all_gather(eddy_state, "row", axis=1, tiled=True),
-        lax.all_gather(eddy_rate, "row", axis=1, tiled=True),
-    )
-    chosen = owners * S + slots
-    lookup = (chosen[:, None] == jnp.arange(owners_total * S, dtype=jnp.int32)[None, :]).astype(
-        jnp.bfloat16
-    )
-    state = jnp.dot(lookup, every_state[0], preferred_element_type=jnp.float32)
-    rates = jnp.dot(lookup, every_rate[0][:, None], preferred_element_type=jnp.float32)[:, 0]
-    forcing_blocks = (rates[:, None] * (state - blocks.astype(jnp.float32))).astype(jnp.bfloat16)
-    coarse = forcing_blocks.reshape(depth, ybands, xbands, components, BY, BX).transpose(
-        3, 0, 1, 4, 2, 5
-    )
-    return coarse.reshape(components, coarse_rows, coarse_cols)
+    )(vel, vort, xt, xc, tab, mix, *small)
+
+
+def filter_tables(rows):
+    taps = np.arange(5 * RATIO) - 2.0 * RATIO - (RATIO - 1) / 2.0
+    value = np.exp(-taps * taps / (8.0 * RATIO * RATIO))
+    value = value / value.sum()
+
+    def weights(offset):
+        inside = (offset >= 0) & (offset < 5 * RATIO)
+        return np.where(inside, value[np.clip(offset, 0, 5 * RATIO - 1)], 0.0).astype(BF16)
+
+    fine = np.arange(256 * RATIO + 256)[:, None] - 128
+    xw = weights(fine - RATIO * np.arange(256)[None, :] + 2 * RATIO)
+    cell = RATIO * np.arange(rows // RATIO)[:, None] - 2 * RATIO
+    yw = weights(np.arange(rows)[None, :] - cell)
+    edge = np.arange(16)[None, :]
+    return xw, yw, weights(edge - 16 - cell), weights(edge + rows - cell)
 
 
 def vertical_inverse_np(planes):
@@ -492,7 +574,12 @@
     n_row, n_col = lax.axis_size("row"), lax.axis_size("col")
     if depth != 1 or not fits(rows, points, n_row, n_col):
         return generic_device(velocity, vorticity, eddy_state, eddy_rate, block_owner, block_slot)
-    coarse = coarse_forcing(velocity, eddy_state, eddy_rate, block_owner, block_slot)
+    held = eddy_state.shape[1]
+    state = eddy_state[0].reshape(held, components * BY, BX).transpose(1, 0, 2)
+    rates = jnp.broadcast_to(eddy_rate[0][None, :, None], (1, held, BX))
+    chosen = (block_owner.reshape(-1) * S + block_slot.reshape(-1)).reshape(-1, points // (RATIO * BX))
+    small = [jnp.concatenate([state, rates], axis=0), jnp.repeat(chosen, BY, axis=0)]
+    small += [jnp.asarray(t) for t in filter_tables(rows)]
     vel = velocity.reshape(components, rows, points)
     vort = vorticity.reshape(components, rows, points)
     xt, xc = (jnp.asarray(t) for t in x_tables_t(points, KXM, n_row))
@@ -507,7 +594,7 @@
     x_wave = lax.axis_index("row") * mode_cols + jnp.arange(mode_cols, dtype=jnp.int32)
     y_wave = lax.axis_index("col") * mode_rows + jnp.arange(mode_rows, dtype=jnp.int32) - KYM // 2
     factor = damping(x_wave, y_wave, NX, NY).reshape(-1)
-    mixed = all_stages(vel, vort, coarse, xt, xc, tab, mix, n_row, n_col)
+    mixed = all_stages(vel, vort, xt, xc, tab, mix, small, n_row, n_col)
     return mixed * factor[None, None, :]
 
 

time: 157 us -> 134 us (0.85)
  blocking collectives: 18.9 us -> 0 us
  matrix products: 11.2 us -> 0 us
  Pallas kernels: 116 us -> 123 us
  other arithmetic: 5.77 us -> 7.78 us
    dot_general x4 -> x0, matrix products: 11.2 us -> none  [the longest x1 7.97 us: coarse_forcing(): jnp.einsum('czyn,nx->czyx', velocity, xweights, preferred_element_type=jn...]
    all_gather x1 -> x0, blocking collectives: 10.3 us -> none  [coarse_forcing(): lax.all_gather(eddy_state, 'row', axis=1, tiled=True)]
    reshape x1 -> x0, blocking collectives: 8.63 us -> none
    pallas_call x1, Pallas kernels: 116 us -> 123 us  [all_stages(): pl.pallas_call(all_kernel, out_shape=jax.ShapeDtypeStruct((3, n_col, line...]
  transfers between devices with their start and end apart: 2 -> 0, of which waited for: 0 -> 0; matrix products, arithmetic and copies ran while one was open for 1% -> 0% of each run, Pallas kernels for 0% -> 0%
where the time goes in v3:
time: 134 us
  Pallas kernels  123 us (92%)
  other arithmetic  7.78 us (6%)
  local copies, waits for them, and re-layouts  3.47 us (3%)
    pallas_call x1, Pallas kernels, all_stages(): pl.pallas_call(all_kernel, out_shape=jax.ShapeDtypeStruct((3, n_col, line...  123 us
    mul x1, other arithmetic, per_device(): return mixed * factor[None, None, :]  5.01 us

profile of v3, /device:TPU:9, one launch (start us, length us, event | category | flops | bytes accessed | tf_op | source)
XLA Modules:
  0.0 134.2 jit_solution(6191247768076565559)
XLA Ops:
  0.0 0.5 broadcast.64
  0.5 1.3 reduce.7
  1.8 0.7 multiply_reduce_fusion
  2.5 0.7 broadcast_in_dim.9
  3.2 0.1 mul.69
  3.3 0.1 reshape.75
  3.4 0.6 broadcast_bitcast_fusion.chosen
  4.1 0.9 copy.16
  5.0 0.7 pad_maximum_fusion.state
  5.6 0.1 multiply_exponential_fusion
  5.7 0.1 broadcast_in_dim.22
  5.9 0.4 mul.78
  6.3 122.9 %all_stages.1 = f32[3,8,51200]{2,1,0:T(8,128)} custom-call(bf16[3,512,2048]{2,1,0:T(8,128)(2,1)} %bitcast.11, bf16[3,512,2048]{2,1,0:T(8,128)(2,1)} %bitcast.12, bf16[1280,2048]{1,0:T(8,128)(2,1)} %constant.39.clone.xt, bf16[1280,512]{1,0:T(8,128)(2,1)} %constant.40.clone.xc, bf16[4,320,1024]{2,1,0:T(8,128)(2,1)} %constant.41.clone.tab, ...), custom_call_target="tpu_custom_call" | custom-call | tf_op jit(solution)/shard_map/all_stages/pallas_call | solution.py:505
  129.2 5.0 %broadcast_multiply_fusion = f32[3,8,51200]{2,1,0:T(8,128)} fusion(f32[3,8,51200]{2,1,0:T(8,128)} %all_stages.1, f32[51200]{0:T(1024)S(1)} %mul.78), kind=kLoop, calls=%fused_computation | loop fusion | flops 1228800 | bytes 10035200 | tf_op jit(solution)/shard_map/mul | solution.py:598
  (3 shorter events, 0.0 us)

commit v4 on v3

--- a/solution.py
+++ b/solution.py
@@ -238,7 +238,7 @@
 
 def all_kernel(
     vel, vort, xt, xc, tab, mix, state, chosen, xw, yw, ytop, ybot, out,
-    velv, vortv, coarsev, along, edges, every, xtv, xcv, tabv, section, repeated, xsend, xrecv, ysend, yrecv, held, done,
+    velv, vortv, coarsev, along, edges, every, picks, rates, xtv, xcv, tabv, section, repeated, xsend, xrecv, ysend, yrecv, held, done,
     load_sem, es_sem, er_sem, ss_sem, sr_sem, xs_sem, xr_sem, ys_sem, yr_sem, out_sem,
 ):
     me, mc = lax.axis_index("row"), lax.axis_index("col")
@@ -254,13 +254,24 @@
         pl.semaphore_signal(
             barrier, inc=1, device_id={"col": lax.rem(mc + d, n_col)}, device_id_type=MESH
         )
-    loads = []
-    for src, dst in (
-        (vel, velv), (vort, vortv), (xt, xtv), (xc, xcv), (tab, tabv),
-    ):
-        loads.append(pltpu.make_async_copy(src, dst, load_sem.at[len(loads)]))
-        loads[-1].start()
-    pl.semaphore_wait(barrier, n_row + n_col - 2)
+    loads = [
+        pltpu.make_async_copy(src, dst, load_sem.at[n])
+        for n, (src, dst) in enumerate(
+            [
+                (vel.at[0], velv.at[0]),
+                (vel.at[1], velv.at[1]),
+                (vel.at[2], velv.at[2]),
+                (vort.at[1], vortv.at[1]),
+                (vort.at[2], vortv.at[2]),
+                (vort.at[0], vortv.at[0]),
+                (xt, xtv),
+                (xc, xcv),
+                (tab, tabv),
+            ]
+        )
+    ]
+    for load in loads[:5]:
+        load.start()
 
     def scopy(d):
         return pltpu.make_async_remote_copy(
@@ -272,24 +283,21 @@
             device_id_type=MESH,
         )
 
-    def ecopy(side):
+    def ecopy(side, comp):
         dest = lax.rem(me + (1 if side == 0 else n_row - 1), n_row)
         lines = slice(rows - 16, rows) if side == 0 else slice(0, 16)
         return pltpu.make_async_remote_copy(
-            src_ref=along.at[:, lines, :],
-            dst_ref=edges.at[side],
-            send_sem=es_sem.at[side],
-            recv_sem=er_sem.at[side],
+            src_ref=along.at[comp, lines, :],
+            dst_ref=edges.at[side, comp],
+            send_sem=es_sem.at[side, comp],
+            recv_sem=er_sem.at[side, comp],
             device_id={"row": dest},
             device_id_type=MESH,
         )
 
-    for d in range(1, n_row):
-        scopy(d).start()
-    loads[0].wait()
     cells = points // RATIO
 
-    def filter_x(comp, carry):
+    def filter_x(comp):
         for h in range(cells // 256):
             low, high = 256 * RATIO * h - 128, 256 * RATIO * h + 256 * RATIO + 128
             cuts = [(max(low, 0), min(high, points), max(-low, 0))]
@@ -305,53 +313,57 @@
                     preferred_element_type=F32,
                 )
             along[comp, :, 256 * h : 256 * (h + 1)] = total.astype(BF16)
-        return carry
-
-    lax.fori_loop(0, 3, filter_x, 0)
-    ecopy(0).start()
-    ecopy(1).start()
+
+    loads[0].wait()
+    filter_x(0)
+    for load in loads[5:]:
+        load.start()
+    pl.semaphore_wait(barrier, n_row + n_col - 2)
+    ecopy(0, 0).start()
+    ecopy(1, 0).start()
+    for d in range(1, n_row):
+        scopy(d).start()
     every[:, me] = state[...]
-    for d in range(1, n_row):
-        source = lax.rem(me + d, n_row)
-        pltpu.make_async_remote_copy(
-            src_ref=state,
-            dst_ref=every.at[:, source],
-            send_sem=ss_sem.at[d - 1],
-            recv_sem=sr_sem.at[source],
-            device_id={"row": source},
-            device_id_type=MESH,
-        ).wait_recv()
-    ecopy(0).wait_recv()
-    ecopy(1).wait_recv()
+    for load in loads[1:5]:
+        load.wait()
     slots = every.shape[1] * every.shape[2]
     lows = rows // RATIO
-    sides = xw.shape[1] // 2
-    smooth = []
-    for comp in range(3):
+
+    def lookups():
+        for d in range(1, n_row):
+            source = lax.rem(me + d, n_row)
+            pltpu.make_async_remote_copy(
+                src_ref=state,
+                dst_ref=every.at[:, source],
+                send_sem=ss_sem.at[d - 1],
+                recv_sem=sr_sem.at[source],
+                device_id={"row": source},
+                device_id_type=MESH,
+            ).wait_recv()
+        deep = lax.broadcasted_iota(jnp.int32, (lows, BY * slots), 1)
+        inner = (lax.broadcasted_iota(jnp.int32, (lows, BY * slots), 0) & (BY - 1)) * slots
+        flat = lax.broadcasted_iota(jnp.int32, (lows, slots), 1)
+        for q in range(cells // BX):
+            name = chosen[:, q : q + 1]
+            picks[q] = jnp.where(deep == inner + name, 1.0, 0.0).astype(BF16)
+            rates[:, q * BX : (q + 1) * BX] = jnp.dot(
+                jnp.where(flat == name, 1.0, 0.0).astype(BF16),
+                every[3 * BY].reshape(slots, BX),
+                preferred_element_type=F32,
+            )
+
+    def force(comp):
+        ecopy(0, comp).wait_recv()
+        ecopy(1, comp).wait_recv()
         total = jnp.dot(yw[...], along[comp], preferred_element_type=F32)
         total += jnp.dot(ytop[...], edges[0, comp], preferred_element_type=F32)
         total += jnp.dot(ybot[...], edges[1, comp], preferred_element_type=F32)
-        smooth.append(total.astype(BF16).astype(F32))
-    deep = lax.broadcasted_iota(jnp.int32, (lows, BY * slots), 1)
-    inner = (lax.broadcasted_iota(jnp.int32, (lows, BY * slots), 0) & (BY - 1)) * slots
-    flat = lax.broadcasted_iota(jnp.int32, (lows, slots), 1)
-    for q in range(cells // BX):
-        name = chosen[:, q : q + 1]
-        pick = jnp.where(deep == inner + name, 1.0, 0.0).astype(BF16)
-        rate = jnp.dot(
-            jnp.where(flat == name, 1.0, 0.0).astype(BF16),
-            every[3 * BY].reshape(slots, BX),
-            preferred_element_type=F32,
-        )
-        for comp in range(3):
-            held_state = jnp.dot(
-                pick,
-                every[comp * BY : (comp + 1) * BY].reshape(BY * slots, BX),
-                preferred_element_type=F32,
-            )
+        smooth = total.astype(BF16).astype(F32)
+        blocks = every[pl.ds(comp * BY, BY)].reshape(BY * slots, BX)
+        for q in range(cells // BX):
             lanes = slice(q * BX, (q + 1) * BX)
-            coarsev[comp, :, lanes] = (rate * (held_state - smooth[comp][:, lanes])).astype(BF16)
-    loads[1].wait()
+            found = jnp.dot(picks[q], blocks, preferred_element_type=F32)
+            coarsev[comp, :, lanes] = (rates[:, lanes] * (found - smooth[:, lanes])).astype(BF16)
 
     far = me // 2
     order = [3 * (1 - far), 2 - far, 1 + 4 * far - me, me]
@@ -380,12 +392,15 @@
             return inner
 
         lax.fori_loop(0, rows // 16, piece, 0)
-        repeated[...] = jnp.dot(spread, coarsev[comp], preferred_element_type=F32).astype(BF16)
 
         @pl.when(comp == 0)
         def _():
-            loads[2].wait()
-            loads[3].wait()
+            lookups()
+            for load in loads[5:8]:
+                load.wait()
+
+        force(comp)
+        repeated[...] = jnp.dot(spread, coarsev[comp], preferred_element_type=F32).astype(BF16)
 
         for k in range(n_row):
             lines = pl.ds(pl.multiple_of(order[k] * width, 16), width)
@@ -396,10 +411,17 @@
                 xcopy(comp, k, order[k]).start()
             else:
                 xrecv[comp, me] = total.astype(BF16)
+
+        @pl.when(comp < 2)
+        def _():
+            filter_x(comp + 1)
+            ecopy(0, comp + 1).start()
+            ecopy(1, comp + 1).start()
+
         return carry
 
     lax.fori_loop(0, 3, xbody, 0)
-    loads[4].wait()
+    loads[8].wait()
 
     def ycopy(comp, d):
         dest = lax.rem(mc + d, n_col)
@@ -484,9 +506,9 @@
     zstage(2)
     for d in range(1, n_row):
         scopy(d).wait_send()
-    ecopy(0).wait_send()
-    ecopy(1).wait_send()
     for comp in range(3):
+        ecopy(0, comp).wait_send()
+        ecopy(1, comp).wait_send()
         pltpu.make_async_copy(done.at[comp], out.at[comp], out_sem.at[comp]).wait()
         for k in range(n_row - 1):
             xcopy(comp, k, order[k]).wait_send()
@@ -514,6 +536,8 @@
             pltpu.VMEM((3, rows, cells), BF16),
             pltpu.VMEM((2, 3, 16, cells), BF16),
             pltpu.VMEM((state[0], n_row, state[1], state[2]), BF16),
+            pltpu.VMEM((cells // BX, rows // RATIO, BY * n_row * state[1]), BF16),
+            pltpu.VMEM((rows // RATIO, cells), F32),
             pltpu.VMEM(xt.shape, BF16),
             pltpu.VMEM(xc.shape, BF16),
             pltpu.VMEM(tab.shape, BF16),
@@ -525,9 +549,9 @@
             pltpu.VMEM((3, n_col, lines, width), BF16),
             pltpu.VMEM((lines, n_col, width), F32),
             pltpu.VMEM((3, n_col, lines * width), F32),
-            dma((5,)),
-            dma((2,)),
-            dma((2,)),
+            dma((9,)),
+            dma((2, 3)),
+            dma((2, 3)),
             dma((n_row,)),
             dma((n_row,)),
             dma((3, n_row)),

time: 134 us -> 137 us (1.022)
  the two profiles are of different devices: /device:TPU:9 before, /device:TPU:17 now
where the time goes in v4:
time: 137 us; the launch traced here: 136 us
  Pallas kernels  125 us (91%)
  other arithmetic  7.78 us (6%)
  local copies, waits for them, and re-layouts  3.47 us (3%)
    pallas_call x1, Pallas kernels, all_stages(): pl.pallas_call(all_kernel, out_shape=jax.ShapeDtypeStruct((3, n_col, line...  125 us
    mul x1, other arithmetic, per_device(): return mixed * factor[None, None, :]  5.01 us

profile of v4, /device:TPU:17, one launch (start us, length us, event | category | flops | bytes accessed | tf_op | source)
XLA Modules:
  0.0 136.4 jit_solution(7453343074487277209)
XLA Ops:
  0.0 0.5 broadcast.64
  0.5 1.3 reduce.7
  1.8 0.7 multiply_reduce_fusion
  2.5 0.7 broadcast_in_dim.9
  3.2 0.1 mul.69
  3.3 0.1 reshape.75
  3.4 0.6 broadcast_bitcast_fusion.chosen
  4.1 0.9 copy.16
  5.0 0.7 pad_maximum_fusion.state
  5.6 0.1 multiply_exponential_fusion
  5.7 0.1 broadcast_in_dim.22
  5.9 0.4 mul.78
  6.3 125.1 %all_stages.1 = f32[3,8,51200]{2,1,0:T(8,128)} custom-call(bf16[3,512,2048]{2,1,0:T(8,128)(2,1)} %bitcast.11, bf16[3,512,2048]{2,1,0:T(8,128)(2,1)} %bitcast.12, bf16[1280,2048]{1,0:T(8,128)(2,1)} %constant.39.clone.xt, bf16[1280,512]{1,0:T(8,128)(2,1)} %constant.40.clone.xc, bf16[4,320,1024]{2,1,0:T(8,128)(2,1)} %constant.41.clone.tab, ...), custom_call_target="tpu_custom_call" | custom-call | tf_op jit(solution)/shard_map/all_stages/pallas_call | solution.py:527
  131.4 5.0 %broadcast_multiply_fusion = f32[3,8,51200]{2,1,0:T(8,128)} fusion(f32[3,8,51200]{2,1,0:T(8,128)} %all_stages.1, f32[51200]{0:T(1024)S(1)} %mul.78), kind=kLoop, calls=%fused_computation | loop fusion | flops 1228800 | bytes 10035200 | tf_op jit(solution)/shard_map/mul | solution.py:622
  (3 shorter events, 0.0 us)

commit v5 on v3

--- a/solution.py
+++ b/solution.py
@@ -237,8 +237,8 @@
 
 
 def all_kernel(
-    vel, vort, xt, xc, tab, mix, state, chosen, xw, yw, ytop, ybot, out,
-    velv, vortv, coarsev, along, edges, every, xtv, xcv, tabv, section, repeated, xsend, xrecv, ysend, yrecv, held, done,
+    vel, vort, xt, xc, tab, mix, eddy, pace, owner, slot, xw, yw, ytop, ybot, out,
+    velv, vortv, coarsev, along, edges, every, state, xtv, xcv, tabv, section, repeated, xsend, xrecv, ysend, yrecv, held, done,
     load_sem, es_sem, er_sem, ss_sem, sr_sem, xs_sem, xr_sem, ys_sem, yr_sem, out_sem,
 ):
     me, mc = lax.axis_index("row"), lax.axis_index("col")
@@ -260,6 +260,9 @@
     ):
         loads.append(pltpu.make_async_copy(src, dst, load_sem.at[len(loads)]))
         loads[-1].start()
+    for v in range(3 * BY):
+        state[v] = eddy[:, v * BX : (v + 1) * BX]
+    state[3 * BY] = pace[...]
     pl.semaphore_wait(barrier, n_row + n_col - 2)
 
     def scopy(d):
@@ -335,8 +338,13 @@
     deep = lax.broadcasted_iota(jnp.int32, (lows, BY * slots), 1)
     inner = (lax.broadcasted_iota(jnp.int32, (lows, BY * slots), 0) & (BY - 1)) * slots
     flat = lax.broadcasted_iota(jnp.int32, (lows, slots), 1)
+    count = owner.shape[1]
+    chosen = jnp.broadcast_to((owner[...] * S + slot[...]).astype(F32), (lows, count))
+    block = lax.broadcasted_iota(jnp.int32, (lows, count), 1)
+    band = lax.broadcasted_iota(jnp.int32, (lows, count), 0) // BY * (cells // BX)
     for q in range(cells // BX):
-        name = chosen[:, q : q + 1]
+        name = jnp.sum(jnp.where(block == band + q, chosen, 0.0), axis=1, keepdims=True)
+        name = name.astype(jnp.int32)
         pick = jnp.where(deep == inner + name, 1.0, 0.0).astype(BF16)
         rate = jnp.dot(
             jnp.where(flat == name, 1.0, 0.0).astype(BF16),
@@ -497,7 +505,7 @@
 def all_stages(vel, vort, xt, xc, tab, mix, small, n_row, n_col):
     _, rows, points = vel.shape
     cells = points // RATIO
-    state = small[0].shape
+    state = (3 * BY + 1, small[0].shape[0], BX)
     width = xt.shape[0] // n_row
     lines = 4 * tab.shape[1] // n_col
     anywhere = pl.BlockSpec(memory_space=pl.ANY)
@@ -514,6 +522,7 @@
             pltpu.VMEM((3, rows, cells), BF16),
             pltpu.VMEM((2, 3, 16, cells), BF16),
             pltpu.VMEM((state[0], n_row, state[1], state[2]), BF16),
+            pltpu.VMEM(state, BF16),
             pltpu.VMEM(xt.shape, BF16),
             pltpu.VMEM(xc.shape, BF16),
             pltpu.VMEM(tab.shape, BF16),
@@ -575,10 +584,12 @@
     if depth != 1 or not fits(rows, points, n_row, n_col):
         return generic_device(velocity, vorticity, eddy_state, eddy_rate, block_owner, block_slot)
     held = eddy_state.shape[1]
-    state = eddy_state[0].reshape(held, components * BY, BX).transpose(1, 0, 2)
-    rates = jnp.broadcast_to(eddy_rate[0][None, :, None], (1, held, BX))
-    chosen = (block_owner.reshape(-1) * S + block_slot.reshape(-1)).reshape(-1, points // (RATIO * BX))
-    small = [jnp.concatenate([state, rates], axis=0), jnp.repeat(chosen, BY, axis=0)]
+    small = [
+        eddy_state[0],
+        jnp.broadcast_to(eddy_rate[0][:, None], (held, BX)),
+        block_owner.reshape(1, -1),
+        block_slot.reshape(1, -1),
+    ]
     small += [jnp.asarray(t) for t in filter_tables(rows)]
     vel = velocity.reshape(components, rows, points)
     vort = vorticity.reshape(components, rows, points)

time: 134 us -> 130 us (0.970)
  other arithmetic: 7.78 us -> 5.12 us
  local copies, waits for them, and re-layouts: 3.47 us -> 1.84 us
    unnamed x2 -> x0, local copies, waits for them, and re-layouts: 1.42 us -> none
where the time goes in v5:
time: 130 us
  Pallas kernels  123 us (95%)
  other arithmetic  5.12 us (4%)
  local copies, waits for them, and re-layouts  1.84 us (1%)
    pallas_call x1, Pallas kernels, all_stages(): pl.pallas_call(all_kernel, out_shape=jax.ShapeDtypeStruct((3, n_col, line...  123 us
    mul x1, other arithmetic, per_device(): return mixed * factor[None, None, :]  5.01 us

profile of v5, /device:TPU:9, one launch (start us, length us, event | category | flops | bytes accessed | tf_op | source)
XLA Modules:
  0.0 129.9 jit_solution(3067753727832622910)
XLA Ops:
  0.0 1.3 %broadcast_in_dim.7.pace = bf16[16,128]{1,0:T(8,128)(2,1)} broadcast(bf16[16]{0:T(256)(128)(2,1)} %bitcast.11), dimensions={0} | broadcast | bytes 4128 | tf_op jit(solution)/shard_map/broadcast_in_dim | solution.py:589
  1.3 0.1 multiply_exponential_fusion
  1.4 0.1 broadcast_in_dim.8
  1.6 0.4 mul.65
  2.0 123.0 %all_stages.1 = f32[3,8,51200]{2,1,0:T(8,128)} custom-call(bf16[3,512,2048]{2,1,0:T(8,128)(2,1)} %bitcast.6, bf16[3,512,2048]{2,1,0:T(8,128)(2,1)} %bitcast.7, bf16[1280,2048]{1,0:T(8,128)(2,1)} %constant.37.clone.xt, bf16[1280,512]{1,0:T(8,128)(2,1)} %constant.38.clone.xc, bf16[4,320,1024]{2,1,0:T(8,128)(2,1)} %constant.39.clone.tab, ...), custom_call_target="tpu_custom_call" | custom-call | tf_op jit(solution)/shard_map/all_stages/pallas_call | solution.py:513
  124.9 5.0 %broadcast_multiply_fusion = f32[3,8,51200]{2,1,0:T(8,128)} fusion(f32[3,8,51200]{2,1,0:T(8,128)} %all_stages.1, f32[51200]{0:T(1024)S(1)} %mul.65), kind=kLoop, calls=%fused_computation | loop fusion | flops 1228800 | bytes 10035200 | tf_op jit(solution)/shard_map/mul | solution.py:609
  (1 shorter events, 0.0 us)
